TPU v7x, 32 devices: a whole 2x2x4 slice. The times are simulated.
32 devices in a mesh: groups: 2 (over y), seq: 4 (over z), heads: 2 (over x), cfg: 2 (over core).
Axes of the slice: x: 2, y: 2, z: 4, core: 2. Of those that a mesh axis runs over, the one named last changes fastest.
Arguments:
- video_tokens: bfloat16 [2, 8, 1152, 1024], P('cfg', ('groups', 'seq'), 'heads'), parts along dimension 1, may hold values from -6 to 6
- text_tokens: bfloat16 [2, 8, 1152, 128], P('cfg', ('groups', 'seq'), 'heads'), parts along dimension 1, may hold values from -6 to 6
- text_length: int32 [2, 8], P('cfg', ('groups', 'seq')), parts along dimension 1, may hold values from 1 to 128
- guide_numer: int32 [8], P(('groups', 'seq')), parts along dimension 0, may hold values from 2 to 8
- guide_denom: int32 [8], P(('groups', 'seq')), parts along dimension 0, may hold values from 4 to 8
- spatial_gain: bfloat16 [1152], replicated, may hold values from 0.25 to 1.75
- spatial_qkv: bfloat16 [3, 1152, 1152], P(None, 'heads'), may hold values from -0.11785113 to 0.11785113
- spatial_out: bfloat16 [1152, 1152], P('heads'), may hold values from -0.1875 to 0.1875
- temporal_gain: bfloat16 [1152], replicated, may hold values from 0.25 to 1.75
- temporal_qkv: bfloat16 [3, 1152, 1152], P(None, 'heads'), may hold values from -0.11785113 to 0.11785113
- temporal_out: bfloat16 [1152, 1152], P('heads'), may hold values from -0.1875 to 0.1875
Outputs:
- guided: bfloat16 [8, 1152, 1024], P(('groups', 'seq'), ('heads', 'cfg')), parts along dimension 0
There are 2 independent parts, one for each index of `groups`. A program takes and returns all parts, laid end to end along the dimension named above; an argument that names none is the same for every part. Nothing has to cross between parts.
Inputs may be any that keep to these rules, and one draw needn't show every extreme that they name: `text_length`: text tokens at or beyond a frame's length are padding.
All inputs are finite; a program needn't handle non-finite values.
Results may differ from a plain program's by a relative error of at most 0.009.
Values may be sent and summed in bfloat16 or wider, within the bound.
No kernel may reach another device: no remote copies, remote signals or barrier semaphores. Data moves between devices by JAX's collectives and lax.ppermute only.
A program may use at most 64 MiB of HBM per device.

v0:
```python
import jax
import jax.numpy as jnp
from jax import lax
from jax.sharding import PartitionSpec as P

D = 1152
HEAD_DIM = 72


epsilon = 1e-06


def from_partner(shard, axis, stride):
    return lax.ppermute(shard, axis, [(i, i ^ 1 << stride) for i in range(lax.axis_size(axis))])


def softmax_along(scores, axis):
    top_score = jnp.max(scores, axis=axis, keepdims=True)
    expons = jnp.exp(scores - top_score)
    return (expons / jnp.sum(expons, axis=axis, keepdims=True)).astype(jnp.bfloat16)


def project_piece(piece, gain_vector, weights, parts):
    gain_piece = gain_vector.astype(jnp.float32)
    weight_piece = weights[parts]
    piece_wide = piece.astype(jnp.float32)
    scaled = (piece_wide * gain_piece[None, :, None]).astype(jnp.bfloat16)
    product = jnp.einsum("kod,fdp->fkop", weight_piece, scaled, preferred_element_type=jnp.float32)
    return (product, jnp.sum(piece_wide * piece_wide, axis=1))


def add_mixed(piece, matrix):
    return jnp.einsum("oc,fcp->fop", matrix, piece, preferred_element_type=jnp.float32)


def shards(
    video_tokens,
    text_tokens,
    text_length,
    guide_numer,
    guide_denom,
    spatial_gain,
    spatial_qkv,
    spatial_out,
    temporal_gain,
    temporal_qkv,
    temporal_out,
):
    frame_count = video_tokens.shape[1]
    width = video_tokens.shape[2]
    positions = video_tokens.shape[3]
    text_count = text_tokens.shape[3]
    local_heads = width // HEAD_DIM
    frame_tokens = video_tokens[0]
    frame_text = text_tokens[0]
    video_piece = lax.all_gather(frame_tokens, "heads", axis=1, tiled=True)
    text_piece = lax.all_gather(frame_text, "heads", axis=1, tiled=True)
    video_add, video_sq = project_piece(video_piece, spatial_gain, spatial_qkv, slice(0, 3))
    text_add, text_sq = project_piece(text_piece, spatial_gain, spatial_qkv, slice(1, 3))
    mixed = (video_add * lax.rsqrt(video_sq / D + epsilon)[:, None, None, :]).astype(jnp.bfloat16)
    mixed = mixed.reshape(frame_count, 3, local_heads, HEAD_DIM, positions)
    context = (text_add * lax.rsqrt(text_sq / D + epsilon)[:, None, None, :]).astype(jnp.bfloat16)
    context = context.reshape(frame_count, 2, local_heads, HEAD_DIM, text_count)
    key_rows = jnp.concatenate([mixed[:, 1], context[:, 0]], axis=3)
    value_rows = jnp.concatenate([mixed[:, 2], context[:, 1]], axis=3)
    query_all = mixed[:, 0]
    text_valid = jnp.arange(text_count, dtype=jnp.int32)[None, :] < text_length[0][:, None]
    valid_keys = jnp.concatenate(
        [jnp.ones((frame_count, positions), dtype=bool), text_valid], axis=1
    )
    block_rows = min(512, positions)
    block_count = positions // block_rows
    frame_ids = jnp.repeat(jnp.arange(frame_count, dtype=jnp.int32), block_count)
    block_ids = jnp.tile(jnp.arange(block_count, dtype=jnp.int32), frame_count)

    def block_step(inputs):
        frame_id, block_id = inputs
        query_rows = lax.dynamic_slice_in_dim(
            query_all[frame_id], block_id * block_rows, block_rows, 2
        )
        scores = jnp.einsum(
            "hep,hek->hpk", query_rows, key_rows[frame_id], preferred_element_type=jnp.float32
        )
        scores = scores * HEAD_DIM ** (-0.5)
        scores = jnp.where(valid_keys[frame_id][None, None, :], scores, -jnp.inf)
        weights = softmax_along(scores, 2)
        result = jnp.einsum(
            "hpk,hek->hep", weights, value_rows[frame_id], preferred_element_type=jnp.float32
        )
        return result.astype(jnp.bfloat16)

    attended = lax.map(block_step, (frame_ids, block_ids))
    attended = attended.reshape(frame_count, block_count, local_heads, HEAD_DIM, block_rows)
    attended = jnp.transpose(attended, (0, 2, 3, 1, 4)).reshape(frame_count, width, positions)
    update = add_mixed(lax.all_gather(attended, "heads", axis=1, tiled=True), spatial_out)
    after_spatial = (frame_tokens.astype(jnp.float32) + update).astype(jnp.bfloat16)
    own_rows = lax.all_to_all(after_spatial, "seq", split_axis=2, concat_axis=0, tiled=True)
    frames_all = own_rows.shape[0]
    columns = own_rows.shape[2]
    piece_add, piece_sq = project_piece(
        lax.all_gather(own_rows, "heads", axis=1, tiled=True),
        temporal_gain,
        temporal_qkv,
        slice(0, 3),
    )
    mixed_time = (piece_add * lax.rsqrt(piece_sq / D + epsilon)[:, None, None, :]).astype(
        jnp.bfloat16
    )
    mixed_time = mixed_time.reshape(frames_all, 3, local_heads, HEAD_DIM, columns)
    time_scores = jnp.einsum(
        "fhep,ghep->hfgp", mixed_time[:, 0], mixed_time[:, 1], preferred_element_type=jnp.float32
    )
    time_weights = softmax_along(time_scores * HEAD_DIM ** (-0.5), 2)
    attended_time = jnp.einsum(
        "hfgp,ghep->fhep", time_weights, mixed_time[:, 2], preferred_element_type=jnp.float32
    )
    attended_time = attended_time.astype(jnp.bfloat16).reshape(frames_all, width, columns)
    update_time = add_mixed(
        lax.all_gather(attended_time, "heads", axis=1, tiled=True), temporal_out
    )
    block_out = (own_rows.astype(jnp.float32) + update_time).astype(jnp.bfloat16)
    returned = lax.all_to_all(block_out, "seq", split_axis=0, concat_axis=2, tiled=True)
    half_width = width // 2
    partner = from_partner(returned, "cfg", 0)
    branch_index = lax.axis_index("cfg")
    cond_full = jnp.where(branch_index == 0, returned, partner)
    uncond_full = jnp.where(branch_index == 0, partner, returned)
    cond_part = lax.dynamic_slice_in_dim(cond_full, branch_index * half_width, half_width, 1)
    uncond_part = lax.dynamic_slice_in_dim(uncond_full, branch_index * half_width, half_width, 1)
    ratio = guide_numer.astype(jnp.float32) / guide_denom.astype(jnp.float32)
    cond_wide = cond_part.astype(jnp.float32)
    uncond_wide = uncond_part.astype(jnp.float32)
    return (uncond_wide + ratio[:, None, None] * (cond_wide - uncond_wide)).astype(jnp.bfloat16)


def solution(mesh):
    return jax.shard_map(
        shards,
        mesh=mesh,
        in_specs=(
            P("cfg", ("groups", "seq"), "heads", None),
            P("cfg", ("groups", "seq"), "heads", None),
            P("cfg", ("groups", "seq")),
            P(("groups", "seq")),
            P(("groups", "seq")),
            P(),
            P(None, "heads", None),
            P("heads", None),
            P(),
            P(None, "heads", None),
            P("heads", None),
        ),
        out_specs=P(("groups", "seq"), ("heads", "cfg"), None),
        check_vma=False,
    )
```

profile of v0, /device:TPU:0, one launch (start us, length us, event | category | flops | bytes accessed | tf_op | source)
XLA Modules:
  0.0 358.9 jit_solution(843548291912899709)
XLA Ops:
  6.5 0.7 all-gather.12.cloned.1.call-update
  7.3 0.7 convert_element_type.98
  8.7 7.7 %all-gather.1 = bf16[1,1,1152,128]{3,2,1,0:T(8,128)(2,1)S(1)} all-gather(bf16[1,1,576,128]{3,2,1,0:T(8,128)(2,1)} %param.14), channel_id=3, replica_groups=mesh['groups'=2,'seq'=4,'heads'=2,'cfg'=2] {'heads'}, dimensions={2}, use_global_device_ids=true | all-gather | bytes 442368 | tf_op jit(solution)/shard_map/all_gather | solution.py:57
  16.4 0.2 fusion.93
  16.6 3.0 fusion.87
  19.6 28.1 %all-gather.12.cloned.1.call-done = bf16[1,1,1152,1024]{3,2,1,0:T(8,128)(2,1)} async-done(((bf16[1,1,576,1024]{3,2,1,0:T(8,128)(2,1)}), bf16[1,1,1152,1024]{3,2,1,0:T(8,128)(2,1)}) %all-gather.12.cloned.1.call-update) | async-done | bytes 2359312 | tf_op jit(solution)/shard_map/all_gather | solution.py:56
  47.7 2.3 fusion.50
  50.1 7.3 %fusion.48 = bf16[1,1024,3,576]{1,3,2,0:T(8,128)(2,1)S(1)} fusion(f32[1024]{0:T(1024)S(1)} %add_rsqrt_fusion.1, bf16[3,576,1152]{2,1,0:T(8,128)(2,1)} %param.19, bf16[1,1,1152,1024]{3,2,1,0:T(8,128)(2,1)S(1)} %copy-done.3, f32[1152]{0:T(1024)S(1)} %convert_element_type.98), kind=kOutput, calls=%fused_computation.28 | convolution fusion | flops 4083941376 | bytes 9888256 | tf_op jit(solution)/shard_map/kod,fdp->fkop/dot_general | solution.py:28
  57.3 1.4 slice_bitcast_fusion
  58.7 1.3 pad_maximum_fusion
  60.1 36.7 %while.10 = (s32[]{:T(128)}, bf16[2,8,72,512]{3,2,1,0:T(8,128)(2,1)}, pred[1,1152]{1,0:T(4,128)(4,1)S(1)}, s32[2]{0:T(128)S(1)}, bf16[1,8,72,1024]{3,2,1,0:T(8,1...) while((s32[]{:T(128)}, ...), condition=%wide.region_5.6_spmd, body=%wide.region_2.5_spmd.sunk | while | flops 2081200384 | bytes 5788856 | solution.py:92
  60.2 0.7 dynamic_slice.50
  61.6 7.0 %exponential_reduce_fusion.2 = f32[8,512]{1,0:T(8,128)S(1)} fusion(pred[1152]{0:T(1024)(128)(4,1)S(1)} %reduce.5, bf16[1,8,72,1152]{3,2,1,0:T(8,128)(2,1)S(1)} %get-tuple-element.139, bf16[1,8,72,1024]{3,2,1,0:T(8,128)(2,1)} %get-tuple-element.138, s32[]{:T(128)S(6)} %select_n.52), kind=kOutput, calls=%fused_computation.5.clone.1 | convolution fusion | flops 698352768 | bytes 1934468 | tf_op jit(solution)/shard_map/while/body/eval_jaxpr/sub | solution.py:19
  68.7 9.8 %fusion.120 = bf16[2,8,72,512]{3,2,1,0:T(8,128)(2,1)} fusion(bf16[2,8,72,512]{3,2,1,0:T(8,128)(2,1)} %get-tuple-element.123, s32[]{:T(128)} %get-tuple-element.122, bf16[1,8,72,1152]{3,2,1,0:T(8,128)(2,1)} %get-tuple-element.140, f32[8,512]{1,0:T(8,128)S(1)} %exponential_reduce_fusion.2, pred[1152]{0:T(1024)(128)(4,1)S(1)} %reduce.5, ...), kind=kOutput, calls=%fused_computation.13.clone.1 | convolution fusion | flops 1382847616 | bytes 3851908 | tf_op jit(solution)/shard_map/while/body/eval_jaxpr/hpk,hek->hep/dot_general | solution.py:87
  78.5 0.7 dynamic_slice.50
  79.9 7.0 %exponential_reduce_fusion.2 = f32[8,512]{1,0:T(8,128)S(1)} fusion(pred[1152]{0:T(1024)(128)(4,1)S(1)} %reduce.5, bf16[1,8,72,1152]{3,2,1,0:T(8,128)(2,1)S(1)} %get-tuple-element.139, bf16[1,8,72,1024]{3,2,1,0:T(8,128)(2,1)} %get-tuple-element.138, s32[]{:T(128)S(6)} %select_n.52), kind=kOutput, calls=%fused_computation.5.clone.1 | convolution fusion | flops 698352768 | bytes 1934468 | tf_op jit(solution)/shard_map/while/body/eval_jaxpr/sub | solution.py:19
  87.0 9.8 %fusion.120 = bf16[2,8,72,512]{3,2,1,0:T(8,128)(2,1)} fusion(bf16[2,8,72,512]{3,2,1,0:T(8,128)(2,1)} %get-tuple-element.123, s32[]{:T(128)} %get-tuple-element.122, bf16[1,8,72,1152]{3,2,1,0:T(8,128)(2,1)} %get-tuple-element.140, f32[8,512]{1,0:T(8,128)S(1)} %exponential_reduce_fusion.2, pred[1152]{0:T(1024)(128)(4,1)S(1)} %reduce.5, ...), kind=kOutput, calls=%fused_computation.13.clone.1 | convolution fusion | flops 1382847616 | bytes 3851908 | tf_op jit(solution)/shard_map/while/body/eval_jaxpr/hpk,hek->hep/dot_general | solution.py:87
  96.8 2.5 copy.43
  99.3 1.7 reshape.105
  101.0 0.3 all-gather.14.cloned.1.call-start
  101.2 35.9 %all-gather.8.cloned.1.call-done = bf16[1,1152,1024]{2,1,0:T(8,128)(2,1)} async-done(((bf16[1,576,1024]{2,1,0:T(8,128)(2,1)}), bf16[1,1152,1024]{2,1,0:T(8,128)(2,1)}) %all-gather.8.cloned.1.call-update) | async-done | bytes 2359312 | tf_op jit(solution)/shard_map/all_gather | solution.py:95
  137.2 3.7 %fusion.64 = bf16[1,576,1024]{2,1,0:T(8,128)(2,1)S(1)} fusion(bf16[576,1152]{1,0:T(8,128)(2,1)S(1)} %copy-done, bf16[1,1152,1024]{2,1,0:T(8,128)(2,1)} %all-gather.8.cloned.1.call-done, bf16[1,1,576,1024]{3,2,1,0:T(8,128)(2,1)} %param.13), kind=kOutput, calls=%fused_computation.47 | convolution fusion | flops 1360723968 | bytes 6045696 | tf_op jit(solution)/shard_map/oc,fcp->fop/dot_general | solution.py:33
  140.8 4.1 %copy.44 = bf16[1,576,1024]{1,0,2:T(2,128)(2,1)} copy(bf16[1,576,1024]{2,1,0:T(8,128)(2,1)S(1)} %fusion.64) | data formatting | bytes 2359296 | tf_op jit(solution)/shard_map/convert_element_type | solution.py:96
  145.0 0.5 broadcast.82
  145.5 9.9 %reduce.3 = bf16[1024,576]{1,0:T(8,128)(2,1)S(1)} reduce(bf16[1024,1,576]{2,1,0:T(2,128)(2,1)} %bitcast.189, bf16[]{:T(256)} %broadcast.82), dimensions={1}, to_apply=%bitcast.164.reduce_sub_computation | reduce | bytes 2359298
  155.4 2.6 reshape.124
  158.0 33.0 %all_to_all.36 = bf16[4,2,73728]{2,1,0:T(2,128)(2,1)S(1)} all-to-all(bf16[4,2,73728]{2,1,0:T(2,128)(2,1)} %reshape.124), channel_id=1, replica_groups=mesh['groups'=2,'seq'=4,'heads'=2,'cfg'=2] {'seq'}, dimensions={0} | all-to-all | bytes 2359296 | tf_op jit(solution)/shard_map/all_to_all | solution.py:97
  191.0 3.3 reshape.125
  194.2 1.9 copy.57
  196.2 1.5 copy.46
  197.7 0.3 all-gather.10.cloned.1.call-start
  198.0 34.0 %all-gather.14.cloned.1.call-done = bf16[4,1,1152,256]{3,2,0,1:T(8,128)(2,1)} async-done(((bf16[4,1,576,256]{3,2,0,1:T(8,128)(2,1)}), bf16[4,1,1152,256]{3,2,0,1:T(8,128)(2,1)}) %all-gather.14.cloned.1.call-update) | async-done | bytes 2359312 | tf_op jit(solution)/shard_map/all_gather | solution.py:101
  232.0 2.3 fusion.52
  234.4 7.2 %multiply_convert_fusion = bf16[4,256,3,576]{1,3,2,0:T(8,128)(2,1)S(1)} fusion(f32[4,256]{1,0:T(4,128)S(1)} %add_rsqrt_fusion, bf16[3,576,1152]{2,1,0:T(8,128)(2,1)} %param.22, bf16[4,1,1152,256]{3,2,0,1:T(8,128)(2,1)S(1)} %copy-done.4, f32[1152]{0:T(1024)S(1)} %convert_element_type.109), kind=kOutput, calls=%fused_computation.29 | convolution fusion | flops 4083941376 | bytes 9888256 | tf_op jit(solution)/shard_map/kod,fdp->fkop/dot_general | solution.py:28
  241.6 1.9 fusion.104
  243.5 2.8 copy.59
  246.4 4.1 %copy.60 = bf16[4,1,8,72,256]{3,0,4,2,1:T(4,128)(2,1)} copy(bf16[4,1,8,72,256]{4,3,2,1,0:T(8,128)(2,1)} %get-tuple-element.59) | data formatting | bytes 2359296
  250.4 5.8 %fusion.71 = f32[8,256,4,4]{3,2,1,0:T(4,128)} fusion(bf16[4,1,8,72,256]{3,0,4,2,1:T(4,128)(2,1)} %copy.60, bf16[4,1,8,72,256]{3,0,4,2,1:T(4,128)(2,1)S(1)} %copy.59), kind=kOutput, calls=%fused_computation.54 | convolution fusion | flops 4718592 | bytes 2490368 | tf_op jit(solution)/shard_map/fhep,ghep->hfgp/dot_general | solution.py:110
  256.2 2.8 copy.50
  259.2 2.1 copy.51
  261.3 2.5 copy.58
  263.8 5.8 %convert_bitcast_fusion = bf16[4,8,72,256]{2,0,3,1:T(4,128)(2,1)} fusion(bf16[8,4,4,256]{2,1,3,0:T(4,128)(2,1)} %copy.51, bf16[4,1,8,72,256]{3,0,4,2,1:T(4,128)(2,1)} %copy.58), kind=kOutput, calls=%fused_computation.59 | convolution fusion | flops 5308416 | bytes 2424832 | tf_op jit(solution)/shard_map/hfgp,ghep->fhep/dot_general | solution.py:114
  269.6 4.2 %copy.52 = bf16[4,8,72,256]{3,2,1,0:T(8,128)(2,1)} copy(bf16[4,8,72,256]{2,0,3,1:T(4,128)(2,1)} %convert_bitcast_fusion) | data formatting | bytes 2359296 | tf_op jit(solution)/shard_map/convert_element_type | solution.py:117
  273.8 36.2 %all-gather.10.cloned.1.call-done = bf16[4,1152,256]{2,1,0:T(8,128)(2,1)} async-done(((bf16[4,576,256]{2,1,0:T(8,128)(2,1)}), bf16[4,1152,256]{2,1,0:T(8,128)(2,1)}) %all-gather.10.cloned.1.call-update) | async-done | bytes 2359312 | tf_op jit(solution)/shard_map/all_gather | solution.py:119
  310.0 3.8 %fusion.63 = bf16[4,576,256]{2,1,0:T(8,128)(2,1)S(1)} fusion(bf16[4,1152,256]{2,1,0:T(8,128)(2,1)} %all-gather.10.cloned.1.call-done, bf16[576,1152]{1,0:T(8,128)(2,1)} %param.23, bf16[1,576,4,256]{3,1,2,0:T(8,128)(2,1)S(1)} %copy-done.2), kind=kOutput, calls=%fused_computation.45 | convolution fusion | flops 1360723968 | bytes 6045696 | tf_op jit(solution)/shard_map/oc,fcp->fop/dot_general | solution.py:33
  313.8 32.8 %all_to_all.37 = bf16[4,576,256]{2,1,0:T(8,128)(2,1)S(1)} all-to-all(bf16[4,576,256]{2,1,0:T(8,128)(2,1)S(1)} %fusion.63), channel_id=1, replica_groups=mesh['groups'=2,'seq'=4,'heads'=2,'cfg'=2] {'seq'}, dimensions={0} | all-to-all | bytes 2359296 | tf_op jit(solution)/shard_map/all_to_all | solution.py:122
  348.1 1.6 collective-permute-done
  349.7 2.2 fusion.91
  (33 shorter events, 0.6 us)
Async XLA Ops:
  6.5 130.6 %copy-start = (bf16[576,1152]{1,0:T(8,128)(2,1)S(1)}, bf16[576,1152]{1,0:T(8,128)(2,1)}, u32[]{:S(2)}) copy-start(bf16[576,1152]{1,0:T(8,128)(2,1)} %param.20) | copy-start | bytes 3981316
  6.5 41.1 %all-gather.12.cloned.1.call-start = ((), (), s32[]{:S(2)}) async-start(), calls=%async_computation.4 | async-start | bytes 3538944 | tf_op jit(solution)/shard_map/all_gather | solution.py:56
  7.3 129.9 %all-gather.8.cloned.1.call-start = ((), (), s32[]{:S(2)}) async-start(), calls=%async_computation.2 | async-start | bytes 3538944 | tf_op jit(solution)/shard_map/all_gather | solution.py:95
  47.7 2.4 copy-start.3
  101.0 131.0 %all-gather.14.cloned.1.call-start = ((), (), s32[]{:S(2)}) async-start(), calls=%async_computation.5 | async-start | bytes 3538944 | tf_op jit(solution)/shard_map/all_gather | solution.py:101
  196.2 1.8 copy-start.5
  197.7 112.3 %all-gather.10.cloned.1.call-start = ((), (), s32[]{:S(2)}) async-start(), calls=%async_computation.3 | async-start | bytes 3538944 | tf_op jit(solution)/shard_map/all_gather | solution.py:119
  232.0 2.4 copy-start.4
  259.1 2.2 copy-start.1
  269.6 40.4 %copy-start.2 = (bf16[1,576,4,256]{3,1,2,0:T(8,128)(2,1)S(1)}, bf16[1,576,4,256]{3,1,2,0:T(8,128)(2,1)}, u32[]{:S(2)}) copy-start(bf16[1,576,4,256]{3,1,2,0:T(8,128)(2,1)} %copy.46) | copy-start | bytes 3538948
  346.7 3.0 collective-permute-start
Sparse Core Ops, SparseCore 0:
  8.9 38.7 all-gather.11
  101.1 36.0 all-gather.7
  197.8 34.1 all-gather.13
  273.9 36.0 all-gather.9
where the time goes:
time: 364 us; the launch traced here: 359 us
  waiting for transfers between devices  137 us (38%)
  blocking collectives  73.5 us (20%)
  matrix products  70.3 us (19%)
  local copies, waits for them, and re-layouts  41.4 us (11%)
  other arithmetic  19.1 us (5%)
  between operations  15.7 us (4%)
    all_gather x1, waiting for transfers between devices, shards(): lax.all_gather(attended_time, 'heads', axis=1, tiled=True)  36.2 us
    all_gather x1, waiting for transfers between devices, shards(): lax.all_gather(attended, 'heads', axis=1, tiled=True)  35.9 us
    all_gather x1, waiting for transfers between devices, shards(): lax.all_gather(own_rows, 'heads', axis=1, tiled=True)  34 us
    all_to_all x1, blocking collectives, shards(): lax.all_to_all(after_spatial, 'seq', split_axis=2, concat_axis=0, tiled=T...  33 us
    all_to_all x1, blocking collectives, shards(): lax.all_to_all(block_out, 'seq', split_axis=0, concat_axis=2, tiled=True)  32.8 us
    all_gather x1, waiting for transfers between devices, shards(): video_piece = lax.all_gather(frame_tokens, 'heads', axis=1, tiled=True)  28.1 us
    dot_general x2, matrix products, block_step(): jnp.einsum('hpk,hek->hep', weights, value_rows[frame_id], preferred_eleme...  19.7 us
    unnamed x19, local copies, waits for them, and re-layouts  17.8 us
  transfers between devices with their start and end apart: 5, of which 5 were waited for; matrix products, arithmetic and copies ran while one was open for 1% of the time, Pallas kernels for 0%

commit v1 on v0

--- a/solution.py
+++ b/solution.py
@@ -1,10 +1,16 @@
+import functools
+
 import jax
 import jax.numpy as jnp
 from jax import lax
+from jax.experimental import pallas as pl
+from jax.experimental.pallas import tpu as pltpu
 from jax.sharding import PartitionSpec as P
 
 D = 1152
 HEAD_DIM = 72
+HEAD_ROWS = 80
+LANES = 128
 
 
 epsilon = 1e-06
@@ -33,7 +39,7 @@
     return jnp.einsum("oc,fcp->fop", matrix, piece, preferred_element_type=jnp.float32)
 
 
-def shards(
+def shards_plain(
     video_tokens,
     text_tokens,
     text_length,
@@ -133,9 +139,573 @@
     return (uncond_wide + ratio[:, None, None] * (cond_wide - uncond_wide)).astype(jnp.bfloat16)
 
 
+def fits(mesh):
+    heads = mesh.shape["heads"]
+    share = mesh.shape["groups"] * mesh.shape["cfg"]
+    return (D // (heads * share)) % (2 * HEAD_DIM) == 0
+
+
+def aligned(offset, step=16):
+    return pl.multiple_of(offset, step)
+
+
+def local(x):
+    return pltpu.with_memory_space_constraint(x, pltpu.VMEM)
+
+
+def resident(kernel, shapes, info, operands, scratch, flops, grant, exps=0, out_local=True):
+    place = pl.BlockSpec(memory_space=pltpu.VMEM)
+    kind = pltpu.VMEM if out_local else jax.ShapeDtypeStruct
+    moved = sum(x.size * x.dtype.itemsize for x in operands)
+    return pl.pallas_call(
+        kernel,
+        out_shape=tuple(kind(shape, dtype) for shape, dtype in shapes),
+        in_specs=[pl.BlockSpec(memory_space=pltpu.SMEM)] + [place] * len(operands),
+        out_specs=(place,) * len(shapes),
+        scratch_shapes=scratch,
+        compiler_params=pltpu.CompilerParams(vmem_limit_bytes=grant << 20),
+        cost_estimate=pl.CostEstimate(flops=flops, bytes_accessed=moved, transcendentals=exps),
+    )(info, *[local(x) for x in operands])
+
+
+def place_of(axis):
+    return lax.axis_index(axis)
+
+
+def base_of(heads, r, width):
+    return lax.rem(place_of("heads") - r + heads, heads) * width
+
+
+def quarter_of(block, rows, groups, cfg):
+    _, dg, dc = block
+    g = lax.rem(place_of("groups") - dg + groups, groups)
+    return (g * cfg + lax.rem(place_of("cfg") - dc + cfg, cfg)) * rows
+
+
+def weave(y, inverse, tail):
+    heads = y.shape[0] // HEAD_DIM
+    y = (y * inverse).reshape(heads, HEAD_DIM, y.shape[1])
+    return jnp.concatenate([y, jnp.broadcast_to(tail, (heads,) + tail.shape)], axis=1)
+
+
+def project_kernel(parts, jobs, info, *refs):
+    inputs, refs = refs[: parts * len(jobs)], refs[parts * len(jobs) :]
+    gain, w, refs = refs[0], refs[1], refs[2:]
+    outs, scaled_refs = refs[: len(jobs)], refs[len(jobs) :]
+    width = w.shape[1]
+    for i, kinds in enumerate(jobs):
+        scaled, total = scaled_refs[i], None
+        for r in range(parts):
+            rows = pl.ds(aligned(base_of(parts, r, width)), width)
+            wide = inputs[i * parts + r][...].astype(jnp.float32)
+            scaled[rows, :] = (wide * gain[rows, :]).astype(jnp.bfloat16)
+            sq = jnp.sum(wide * wide, axis=0, keepdims=True)
+            total = sq if total is None else total + sq
+        inverse = lax.rsqrt(total / D + epsilon)
+        row = lax.broadcasted_iota(
+            jnp.int32, (HEAD_ROWS - HEAD_DIM, scaled.shape[1]), 0
+        )
+        for slot, kind in enumerate(kinds):
+            y = jnp.dot(w[kind], scaled[...], preferred_element_type=jnp.float32)
+            tail = jnp.where((row == 0) & (kind == 2), 1.0, 0.0)
+            outs[i][slot] = weave(y, inverse, tail).astype(jnp.bfloat16)
+
+
+def project_call(info, sets, jobs, gain, w):
+    width = w.shape[1]
+    heads = width // HEAD_DIM
+    parts = len(sets[0])
+    counts = [x[0].shape[1] for x in sets]
+    shapes = [
+        ((len(kinds), heads, HEAD_ROWS, n), jnp.bfloat16) for kinds, n in zip(jobs, counts)
+    ]
+    return resident(
+        functools.partial(project_kernel, parts, jobs),
+        shapes,
+        info,
+        [x for group in sets for x in group] + [gain, w],
+        [pltpu.VMEM((D, n), jnp.bfloat16) for n in counts],
+        6 * width * D * sum(counts),
+        12,
+    )
+
+
+def attend_kernel(n, heads_axis, ahead, info, *refs):
+    chunks, (text, out, s_buf, m_buf, o_buf) = refs[:n], refs[n:]
+    heads, block = chunks[0].shape[1], chunks[0].shape[3]
+    per = out.shape[1] // block
+    half = lax.rem(place_of("heads") + ahead, heads_axis)
+    rate = HEAD_DIM ** (-0.5) * 1.4426950408889634
+    contract = (((0,), (0,)), ((), ()))
+
+    def fold(s):
+        return jnp.max(s.reshape(s.shape[0] // 8, 8, s.shape[1]), axis=0)
+
+    def score(head, j, slot):
+        q = chunks[j][0, head]
+        for b in range(1, heads_axis):
+            q = jnp.where(half == b, chunks[b * per + j][0, head], q)
+        top = None
+        for i, chunk in enumerate(chunks):
+            s = lax.dot_general(chunk[1, head], q, contract, preferred_element_type=jnp.float32)
+            s_buf[slot, i * block : (i + 1) * block, :] = s
+            top = fold(s) if top is None else jnp.maximum(top, fold(s))
+        t = lax.dot_general(text[0, head], q, contract, preferred_element_type=jnp.float32)
+        live = lax.broadcasted_iota(jnp.int32, t.shape, 0) < info[0]
+        t = jnp.where(live, t, -jnp.inf)
+        s_buf[slot, n * block :, :] = t
+        m_buf[slot] = jnp.maximum(top, fold(t))
+
+    def mix(head, j, slot):
+        top = jnp.max(m_buf[slot], axis=0, keepdims=True)
+        o = None
+        for i in range(n + 1):
+            if i < n:
+                s, v = s_buf[slot, i * block : (i + 1) * block, :], chunks[i][2, head]
+            else:
+                s, v = s_buf[slot, n * block :, :], text[1, head]
+            e = jnp.exp2((s - top) * rate).astype(jnp.bfloat16)
+            term = jnp.dot(v, e, preferred_element_type=jnp.float32)
+            o = term if o is None else o + term
+        rows = pl.ds(aligned(head * HEAD_DIM, 8), HEAD_DIM)
+        o_buf[rows, j * block : (j + 1) * block] = o[:HEAD_DIM] / o[HEAD_DIM : HEAD_DIM + 1]
+
+    score(0, 0, 0)
+
+    def step(head, carry):
+        for j in range(per):
+            if j + 1 < per:
+                score(head, j + 1, (j + 1) % 2)
+            else:
+                score(head + 1, 0, 0)
+            mix(head, j, j % 2)
+        return carry
+
+    lax.fori_loop(0, heads - 1, step, 0)
+    for j in range(per):
+        if j + 1 < per:
+            score(heads - 1, j + 1, (j + 1) % 2)
+        mix(heads - 1, j, j % 2)
+    out[...] = o_buf[...].astype(jnp.bfloat16)
+
+
+def attend_call(info, chunks, text, heads_axis, ahead):
+    _, heads, _, block = chunks[0].shape
+    count = block * len(chunks) // heads_axis
+    keys = block * len(chunks) + text.shape[3]
+    return resident(
+        functools.partial(attend_kernel, len(chunks), heads_axis, ahead),
+        [((heads * HEAD_DIM, count), jnp.bfloat16)],
+        info,
+        list(chunks) + [text],
+        [
+            pltpu.VMEM((2, keys, block), jnp.float32),
+            pltpu.VMEM((2, 8, block), jnp.float32),
+            pltpu.VMEM((heads * HEAD_DIM, count), jnp.float32),
+        ],
+        4 * heads * 256 * count * keys,
+        8,
+        heads * count * keys,
+    )[0]
+
+
+def out_kernel(n, per, extra, seq, blocks, share, info, *refs):
+    att, refs = refs[:n], refs[n:]
+    tokens, refs = refs[: per * n * len(blocks)], refs[per * n * len(blocks) :]
+    w, refs = refs[: len(blocks)], refs[len(blocks) :]
+    outs, (a, held) = refs[:seq], refs[seq:]
+    width = att[0].shape[0]
+    lanes = outs[0].shape[1]
+    block = tokens[0].shape[1]
+    half, frame = place_of("heads"), place_of("seq")
+    for r in range(n):
+        a[pl.ds(aligned(base_of(n, r, width)), width), :] = att[r][...]
+    for b, key in enumerate(blocks):
+        y = jnp.dot(w[b][...], a[...], preferred_element_type=jnp.float32)
+        count = y.shape[0]
+        if count == width:
+            inner, rows = slice(0, width), slice(0, width)
+        else:
+            offset = aligned(quarter_of(key, count, *share))
+            inner, rows = pl.ds(offset, count), pl.ds(aligned((key[0] - 1) * width + offset), count)
+        for j in range(per):
+            x = tokens[(b * n) * per + j][inner, :]
+            for i in range(1, n):
+                x = jnp.where(half == i, tokens[(b * n + i) * per + j][inner, :], x)
+            cols = slice(j * block, (j + 1) * block)
+            held[rows, cols] = (x.astype(jnp.float32) + y[:, cols]).astype(jnp.bfloat16)
+    total = held.shape[0]
+    for k in range(seq):
+        dest = lax.rem(frame + k, seq)
+        outs[k][0:total, :] = held[:, pl.ds(aligned(dest * lanes, LANES), lanes)]
+        if extra:
+            row = lax.broadcasted_iota(jnp.int32, (extra, lanes), 0)
+            numer, denom = info[1].astype(jnp.float32), info[2].astype(jnp.float32)
+            tail = jnp.where(row == 0, numer, jnp.where(row == 1, denom, 0.0))
+            outs[k][total:, :] = tail.astype(jnp.bfloat16)
+
+
+def out_call(info, att, tokens, w, per, extra, seq, total, blocks, share):
+    n = len(att)
+    count = att[0].shape[1]
+    return resident(
+        functools.partial(out_kernel, n, per, extra, seq, blocks, share),
+        [((total + extra, count // seq), jnp.bfloat16)] * seq,
+        info,
+        list(att) + [x for group in tokens for x in group] + list(w),
+        [pltpu.VMEM((D, count), jnp.bfloat16), pltpu.VMEM((total, count), jnp.bfloat16)],
+        2 * D * total * count,
+        12,
+    )
+
+
+def time_kernel(frames, parts, groups, cfg, keys, info, *refs):
+    blocks, share = len(keys), groups * cfg
+    near, refs = refs[:frames], refs[frames:]
+    far, refs = refs[:frames], refs[frames:]
+    gain, w_own, o_own, refs = refs[0], refs[1], refs[2], refs[3:]
+    w_far, refs = refs[: 3 * blocks], refs[3 * blocks :]
+    o_far, refs = refs[:blocks], refs[blocks:]
+    keep, send, ratios, xs, att, res = refs
+    lanes = near[0].shape[1]
+    width = w_own.shape[1]
+    rows = width // share
+    heads = rows // HEAD_DIM
+    head_index, branch = place_of("heads"), place_of("cfg")
+    offsets = [base_of(parts, 0, width) + q * rows for q in range(share)]
+    offsets += [
+        base_of(parts, key[0], width) + quarter_of(key, rows, groups, cfg) for key in keys
+    ]
+
+    def w_of(b, kind):
+        if b < share:
+            return w_own[kind, b * rows : (b + 1) * rows, :]
+        return w_far[3 * (b - share) + kind][...]
+
+    def o_of(b):
+        if b < share:
+            return o_own[b * rows : (b + 1) * rows, :]
+        return o_far[b - share][...]
+
+    inverses = []
+    for f in range(frames):
+        cols = slice(f * lanes, (f + 1) * lanes)
+        total = None
+        for r in range(parts):
+            base = base_of(parts, r, width)
+            span = pl.ds(aligned(base), width)
+            if r == 0:
+                x = near[f][0:width, :]
+            else:
+                x = far[f][(r - 1) * width : r * width, :]
+            res[f, span, :] = x
+            x = x.astype(jnp.float32)
+            xs[span, cols] = (x * gain[pl.ds(aligned(D + base), width), :]).astype(jnp.bfloat16)
+            sq = jnp.sum(x * x, axis=0, keepdims=True)
+            total = sq if total is None else total + sq
+        inverses.append(lax.rsqrt(total / D + epsilon))
+        tail = near[f][width:, :].astype(jnp.float32)
+        ratios[f : f + 1, :] = tail[0:1] / tail[1:2]
+    inverse = jnp.concatenate(inverses, axis=1)
+
+    for b in range(share + blocks):
+        split = []
+        for kind in range(3):
+            y = jnp.dot(w_of(b, kind), xs[...], preferred_element_type=jnp.float32)
+            y = (y * inverse).astype(jnp.bfloat16).astype(jnp.float32)
+            split.append(
+                [
+                    y[:, f * lanes : (f + 1) * lanes].reshape(heads, HEAD_DIM, lanes)
+                    for f in range(frames)
+                ]
+            )
+        query, key, value = split
+        for f in range(frames):
+            scores = [
+                jnp.sum(query[f] * key[g], axis=1, keepdims=True) * HEAD_DIM ** (-0.5)
+                for g in range(frames)
+            ]
+            top = functools.reduce(jnp.maximum, scores)
+            expons = [jnp.exp(x - top) for x in scores]
+            bottom = functools.reduce(jnp.add, expons)
+            result = None
+            for g in range(frames):
+                weight = (expons[g] / bottom).astype(jnp.bfloat16).astype(jnp.float32)
+                term = weight * value[g]
+                result = term if result is None else result + term
+            att[pl.ds(aligned(offsets[b]), rows), f * lanes : (f + 1) * lanes] = (
+                result.reshape(rows, lanes).astype(jnp.bfloat16)
+            )
+
+    for b in range(share + blocks):
+        y = jnp.dot(o_of(b), att[...], preferred_element_type=jnp.float32)
+        span = pl.ds(aligned(offsets[b]), rows)
+        for f in range(frames):
+            x = res[f, span, :].astype(jnp.float32) + y[:, f * lanes : (f + 1) * lanes]
+            res[f, span, :] = x.astype(jnp.bfloat16)
+
+    slot = keep.shape[2]
+    for f in range(frames):
+        for r in range(parts):
+            head = lax.rem(head_index + r, parts)
+            keep[f, r] = res[f, pl.ds(aligned((head * 2 + branch) * slot), slot), :]
+            send[f, r] = res[f, pl.ds(aligned((head * 2 + 1 - branch) * slot), slot), :]
+
+
+def time_call(info, near, far, gain, w_own, o_own, w_far, o_far, parts, groups, cfg, keys):
+    frames, lanes = len(near), near[0].shape[1]
+    result = ((frames, parts, D // (2 * parts), lanes), jnp.bfloat16)
+    return resident(
+        functools.partial(time_kernel, frames, parts, groups, cfg, keys),
+        [result, result, ((frames, lanes), jnp.float32)],
+        info,
+        list(near) + list(far) + [gain, w_own, o_own] + list(w_far) + list(o_far),
+        [
+            pltpu.VMEM((D, frames * lanes), jnp.bfloat16),
+            pltpu.VMEM((D, frames * lanes), jnp.bfloat16),
+            pltpu.VMEM((frames, D, lanes), jnp.bfloat16),
+        ],
+        8 * D * D * frames * lanes,
+        12,
+    )
+
+
+def guide_kernel(info, keep, other, ratios, *outs):
+    frames, parts = keep.shape[0], keep.shape[1]
+    branch = place_of("cfg")
+    for f in range(frames):
+        ratio = ratios[f : f + 1, :]
+        for r in range(parts):
+            mine = keep[f, r].astype(jnp.float32)
+            theirs = other[f, r].astype(jnp.float32)
+            cond = jnp.where(branch == 0, mine, theirs)
+            uncond = jnp.where(branch == 0, theirs, mine)
+            outs[f * parts + r][...] = (uncond + ratio * (cond - uncond)).astype(jnp.bfloat16)
+
+
+def place_kernel(seq, parts, info, *refs):
+    out = refs[seq * parts]
+    head, frame = place_of("heads"), place_of("seq")
+    for k in range(seq):
+        for r in range(parts):
+            piece = refs[k * parts + r]
+            slot = lax.rem(head - r + parts, parts) * seq + lax.rem(frame + k, seq)
+            lanes = piece.shape[1]
+            out[:, pl.ds(aligned(slot * lanes, LANES), lanes)] = piece[...]
+
+
+def pick_kernel(groups, cfg, *refs):
+    count = len(refs) // 2
+    sources, outs, sems = refs[:count], refs[count : 2 * count], refs[2 * count]
+    copies = []
+    for i, (source, out) in enumerate(zip(sources, outs)):
+        rows = out.shape[-2]
+        span = pl.ds(aligned(quarter_of((0, 0, 0), rows, groups, cfg)), rows)
+        view = source.at[:, span, :] if len(source.shape) == 3 else source.at[span, :]
+        copies.append(pltpu.make_async_copy(view, out, sems.at[i]))
+    for copy in copies:
+        copy.start()
+    for copy in copies:
+        copy.wait()
+
+
+def shift(x, axis, by):
+    size = lax.axis_size(axis)
+    return lax.ppermute(x, axis, [(i, (i + by) % size) for i in range(size)])
+
+
+def after(x, *gates):
+    return lax.optimization_barrier((x,) + gates)[0]
+
+
+def shards(fit, *args):
+    (video_tokens, _, _, _, _, _, _, _, _, _, _) = args
+    heads, seq = lax.axis_size("heads"), lax.axis_size("seq")
+    positions = video_tokens.shape[3]
+    lanes = positions // (heads * seq)
+    if not fit or lanes % LANES or seq % 2 or video_tokens.shape[1] != 1:
+        return shards_plain(*args)
+    return shards_fast(*args)
+
+
+def shards_fast(
+    video_tokens,
+    text_tokens,
+    text_length,
+    guide_numer,
+    guide_denom,
+    spatial_gain,
+    spatial_qkv,
+    spatial_out,
+    temporal_gain,
+    temporal_qkv,
+    temporal_out,
+):
+    heads, seq = lax.axis_size("heads"), lax.axis_size("seq")
+    groups, cfg = lax.axis_size("groups"), lax.axis_size("cfg")
+    positions = video_tokens.shape[3]
+    lanes = positions // (heads * seq)
+    video, text = video_tokens[0, 0], text_tokens[0, 0]
+    width = video.shape[0]
+    rows = width // (groups * cfg)
+    per = 2
+    block = positions // (heads * per)
+    ring = range(1, heads)
+    info = jnp.concatenate([text_length[0], guide_numer, guide_denom])
+    gain = jnp.concatenate([spatial_gain, temporal_gain]).astype(jnp.float32)[:, None]
+
+    text_set = [text] + [shift(text, "heads", r) for r in ring]
+    chunk_sets = []
+    for j in range(heads * per):
+        part = video[:, j * block : (j + 1) * block]
+        chunk_sets.append([part] + [shift(part, "heads", r) for r in ring])
+
+    anywhere = pl.BlockSpec(memory_space=pl.ANY)
+    sources = [spatial_out, temporal_qkv, temporal_out]
+    mine_out, mine_time, mine_last = pl.pallas_call(
+        functools.partial(pick_kernel, groups, cfg),
+        out_shape=(
+            jax.ShapeDtypeStruct((rows, D), jnp.bfloat16),
+            jax.ShapeDtypeStruct((3, rows, D), jnp.bfloat16),
+            jax.ShapeDtypeStruct((rows, D), jnp.bfloat16),
+        ),
+        in_specs=[anywhere] * 3,
+        out_specs=(pl.BlockSpec(memory_space=pltpu.VMEM),) * 3,
+        scratch_shapes=[pltpu.SemaphoreType.DMA((3,))],
+        compiler_params=pltpu.CompilerParams(vmem_limit_bytes=8 << 20),
+    )(*sources)
+
+    chunks = []
+    for j, chunk in enumerate(chunk_sets):
+        if j == 0:
+            text_kv, made = project_call(
+                info, [text_set, chunk], [(1, 2), (0, 1, 2)], gain, spatial_qkv
+            )
+        else:
+            ready = [chunk[0]] + [after(x, chunks[-1]) for x in chunk[1:]]
+            (made,) = project_call(info, [ready], [(0, 1, 2)], gain, spatial_qkv)
+        chunks.append(made)
+
+    keys = [(r, dg, dc) for r in ring for dg in range(groups) for dc in range(cfg)]
+
+    def first_hop(mine, gate):
+        mine = after(mine, gate)
+        return {(r, 0, 0): shift(mine, "heads", r) for r in ring}
+
+    def second_hop(held, gate):
+        for r in ring:
+            for dg in range(1, groups):
+                source = after(held[r, 0, 0], gate)
+                held[r, dg, 0] = shift(source, "groups", dg)
+
+    def third_hop(held, gate):
+        for r in ring:
+            for dg in range(groups):
+                for dc in range(1, cfg):
+                    source = after(held[r, dg, 0], gate)
+                    held[r, dg, dc] = shift(source, "cfg", dc)
+
+    arrived = chunk_sets[-1][-1]
+    far_out = first_hop(mine_out, arrived)
+    far_time = [first_hop(mine_time[0], arrived)]
+
+    att = {}
+    for r in ring:
+        att[r] = attend_call(info, chunks, text_kv, heads, r)
+    mark = att[heads - 1]
+    for r in ring:
+        att[r] = shift(att[r], "heads", r)
+    far_time.append(first_hop(mine_time[1], mark))
+    second_hop(far_out, mark)
+    second_hop(far_time[0], mark)
+    att[0] = attend_call(info, chunks, text_kv, heads, 0)
+    third_hop(far_out, att[0])
+    att_all = [att[r] for r in range(heads)]
+
+    def held_tokens(r):
+        return [x[r] for x in chunk_sets]
+
+    split = (groups, cfg)
+    near = out_call(
+        info, att_all, [held_tokens(0)], [spatial_out], per, 16, seq, width, [(0, 0, 0)], split
+    )
+    far = out_call(
+        info,
+        att_all,
+        [held_tokens(key[0]) for key in keys],
+        [far_out[key] for key in keys],
+        per,
+        0,
+        seq,
+        D - width,
+        keys,
+        split,
+    )
+    far_time.append(first_hop(mine_time[2], near[0]))
+    far_last = first_hop(mine_last, near[0])
+    third_hop(far_time[0], far[0])
+    second_hop(far_time[1], far[0])
+    third_hop(far_time[1], far[0])
+    second_hop(far_time[2], far[0])
+    second_hop(far_last, far[0])
+    third_hop(far_time[2], far[0])
+    third_hop(far_last, far[0])
+    near = [near[0]] + [shift(near[k], "seq", k) for k in range(1, seq)]
+    far = [far[0]] + [shift(far[k], "seq", k) for k in range(1, seq)]
+
+    keep, send, ratios = time_call(
+        info,
+        near,
+        far,
+        gain,
+        temporal_qkv,
+        temporal_out,
+        [far_time[kind][key] for key in keys for kind in range(3)],
+        [far_last[key] for key in keys],
+        heads,
+        groups,
+        cfg,
+        keys,
+    )
+    other = shift(send, "cfg", 1)
+    slot = D // (heads * cfg)
+    pieces = resident(
+        guide_kernel,
+        [((slot, lanes), jnp.bfloat16)] * (seq * heads),
+        info,
+        [keep, other, ratios],
+        [],
+        seq * D * lanes,
+        8,
+    )
+    landed = []
+    for k in range(seq):
+        for r in range(heads):
+            piece = pieces[k * heads + r]
+            if k or r:
+                route = [
+                    (a * heads + b, (a - k) % seq * heads + (b + r) % heads)
+                    for a in range(seq)
+                    for b in range(heads)
+                ]
+                piece = lax.ppermute(piece, ("seq", "heads"), route)
+            landed.append(piece)
+    (result,) = resident(
+        functools.partial(place_kernel, seq, heads),
+        [((slot, positions), jnp.bfloat16)],
+        info,
+        landed,
+        [],
+        0,
+        8,
+        out_local=False,
+    )
+    return result[None]
+
+
 def solution(mesh):
     return jax.shard_map(
-        shards,
+        functools.partial(shards, fits(mesh)),
         mesh=mesh,
         in_specs=(
             P("cfg", ("groups", "seq"), "heads", None),

time: 364 us -> 167 us (0.46); the launches traced: 359 us -> 167 us
  blocking collectives: 73.5 us -> 0 us
  matrix products: 70.3 us -> 0 us
  waiting for transfers between devices: 137 us -> 78 us
  starting transfers between devices: 0.66 us -> 39.8 us
  Pallas kernels: 0 us -> 38.9 us
  local copies, waits for them, and re-layouts: 41.4 us -> 6.68 us
  other arithmetic: 19.1 us -> 1.23 us
  between operations: 15.7 us -> 2.16 us
    all_gather x4 -> x0, waiting for transfers between devices: 134 us -> none  [the longest x1 36.2 us: shards(): lax.all_gather(attended_time, 'heads', axis=1, tiled=True)]
    ppermute x1 -> x40, waiting for transfers between devices: 1.62 us -> 78 us  [the longest x33 70.4 us: shift(): return lax.ppermute(x, axis, [(i, (i + by) % size) for i in range(size)])]
    all_to_all x2 -> x0, blocking collectives: 65.7 us -> none  [the longest x1 33 us: shards(): lax.all_to_all(after_spatial, 'seq', split_axis=2, concat_axis=0, tiled=T...]
    dot_general x9 -> x0, matrix products: 56.2 us -> none  [the longest x2 19.7 us: block_step(): jnp.einsum('hpk,hek->hep', weights, value_rows[frame_id], preferred_eleme...]
    ppermute x1 -> x40, starting transfers between devices: 0.07 us -> 39.8 us  [the longest x33 29.6 us: shift(): return lax.ppermute(x, axis, [(i, (i + by) % size) for i in range(size)])]
    pallas_call x0 -> x12, Pallas kernels: none -> 38.9 us  [the longest x11 38.6 us: resident(): pl.pallas_call(kernel, out_shape=tuple((kind(shape, dtype) for shape, dty...]
    unnamed x19 -> x18, local copies, waits for them, and re-layouts: 17.8 us -> 3.47 us
    sub x2 -> x0, matrix products: 14.1 us -> none  [softmax_along(): expons = jnp.exp(scores - top_score)]
  transfers between devices with their start and end apart: 5 -> 40, of which waited for: 5 -> 19; matrix products, arithmetic and copies ran while one was open for 1% -> 3% of each run, Pallas kernels for 0% -> 11%
where the time goes in v1:
time: 167 us
  waiting for transfers between devices  78 us (47%)
  starting transfers between devices  39.8 us (24%)
  Pallas kernels  38.9 us (23%)
  local copies, waits for them, and re-layouts  6.68 us (4%)
  between operations  2.16 us (1%)
    ppermute x33, waiting for transfers between devices, shift(): return lax.ppermute(x, axis, [(i, (i + by) % size) for i in range(size)])  70.4 us
    pallas_call x11, Pallas kernels, resident(): pl.pallas_call(kernel, out_shape=tuple((kind(shape, dtype) for shape, dty...  38.6 us
    ppermute x33, starting transfers between devices, shift(): return lax.ppermute(x, axis, [(i, (i + by) % size) for i in range(size)])  29.6 us
    ppermute x7, starting transfers between devices, shards_fast(): piece = lax.ppermute(piece, ('seq', 'heads'), route)  10.2 us
    ppermute x7, waiting for transfers between devices, shards_fast(): piece = lax.ppermute(piece, ('seq', 'heads'), route)  7.56 us
    unnamed x18, local copies, waits for them, and re-layouts  3.47 us
  transfers between devices with their start and end apart: 40, of which 19 were waited for; matrix products, arithmetic and copies ran while one was open for 3% of the time, Pallas kernels for 11%

profile of v1, /device:TPU:0, one launch (start us, length us, event | category | flops | bytes accessed | tf_op | source)
XLA Modules:
  0.0 166.8 jit_solution(4418709917694940372)
XLA Ops:
  0.0 3.0 %collective-permute-start = (bf16[576,128]{1,0:T(8,128)(2,1)}, bf16[576,128]{1,0:T(8,128)(2,1)S(1)}, u32[]{:S(2)}, u32[]{:S(2)}) collective-permute-start(bf16[576,128]{1,0:T(8,128)(2,1)} %bitcast.11), channel_id=1, source_target_pairs={{0,2},{2,0},{1,3},{3,1},{4,6},{6,4},{5,7},{7,5},{8,10},{10,8},{9,1... | collective-permute-start | bytes 442376 | tf_op jit(solution)/shard_map/ppermute | solution.py:514
  3.0 2.0 %fusion = (bf16[576,256]{1,0:T(8,128)(2,1)S(1)}, bf16[576,256]{1,0:T(8,128)(2,1)S(1)}, bf16[576,256]{1,0:T(8,128)(2,1)}, bf16[576,256]{1,0:T(8,128)(2,1)S(1)}) fusion(bf16[576,1024]{1,0:T(8,128)(2,1)} %bitcast.13), kind=kLoop, calls=%fused_computation.5 | loop fusion | bytes 2359296 | tf_op jit(solution)/shard_map/slice | solution.py:560
  5.0 2.0 %collective-permute-start.3 = (bf16[576,256]{1,0:T(8,128)(2,1)S(1)}, bf16[576,256]{1,0:T(8,128)(2,1)S(1)}, u32[]{:S(2)}, u32[]{:S(2)}) collective-permute-start(bf16[576,256]{1,0:T(8,128)(2,1)S(1)} %get-tuple-element.94.refs_0_.refs_4_), channel_id=1, source_target_pairs={{0,2},{2,0},{1,3},{3,1},{4,6},{6,4},{5,7},{7,5},{8,10},{10,8},{9,1... | collective-permute-start | bytes 884744 | tf_op jit(solution)/shard_map/ppermute | solution.py:514
  7.0 2.0 %collective-permute-start.1 = (bf16[576,256]{1,0:T(8,128)(2,1)S(1)}, bf16[576,256]{1,0:T(8,128)(2,1)S(1)}, u32[]{:S(2)}, u32[]{:S(2)}) collective-permute-start(bf16[576,256]{1,0:T(8,128)(2,1)S(1)} %get-tuple-element.96.refs_2_), channel_id=1, source_target_pairs={{0,2},{2,0},{1,3},{3,1},{4,6},{6,4},{5,7},{7,5},{8,10},{10,8},{9,1... | collective-permute-start | bytes 884744 | tf_op jit(solution)/shard_map/ppermute | solution.py:514
  11.1 1.1 copy.14
  12.2 1.1 convert_element_type.10.refs_4_.refs_2_.refs_8_
  13.4 2.1 %copy-done.2 = bf16[3,576,1152]{2,1,0:T(8,128)(2,1)S(1)} copy-done((bf16[3,576,1152]{2,1,0:T(8,128)(2,1)S(1)}, bf16[3,576,1152]{2,1,0:T(8,128)(2,1)}, u32[]{:S(2)}) %copy-start.2) | copy-done | bytes 3981336
  15.5 1.3 copy-done.4
  17.2 15.2 %collective-permute-done.1.refs_3_.refs_2_.refs_6_.refs_10_.refs_14_ = bf16[576,256]{1,0:T(8,128)(2,1)S(1)} collective-permute-done((bf16[576,256]{1,0:T(8,128)(2,1)S(1)}, bf16[576,256]{1,0:T(8,128)(2,1)S(1)}, u32[]{:S(2)}, u32[]{:S(2)}) %collective-permute-start.1) | collective-permute-done | bytes 294944 | tf_op jit(solution)/shard_map/ppermute | solution.py:514
  32.4 2.8 %shard_map.109 = (bf16[2,8,80,128]{3,2,1,0:T(8,128)(2,1)S(1)}, bf16[3,8,80,256]{3,2,1,0:T(8,128)(2,1)S(1)}) custom-call(s32[3]{0:T(128)S(1)} %pad_add_fusion.info, bf16[576,128]{1,0:T(8,128)(2,1)S(1)} %bitcast.12, bf16[576,128]{1,0:T(8,128)(2,1)S(1)} %collective-permute-done.refs_1_, bf16[576,256]{1,0:T(8,128)(2,1)S(1)} %get-tuple-element.96.refs_2_, ...), custom_call_target="tpu_custom_call" | custom-call | flops 1528823808 | bytes 4875264 | tf_op jit(solution)/shard_map/pallas_call | solution.py:160
  35.3 2.5 %shard_map.110.refs_1_ = bf16[3,8,80,256]{3,2,1,0:T(8,128)(2,1)S(1)} custom-call(s32[3]{0:T(128)S(1)} %pad_add_fusion.info, bf16[576,256]{1,0:T(8,128)(2,1)} %get-tuple-element.95.refs_0_.refs_3_, bf16[576,256]{1,0:T(8,128)(2,1)S(1)} %collective-permute-done.2.refs_1_.refs_3_.refs_7_.refs_11_.refs_15_, ...), custom_call_target="tpu_custom_call" | custom-call | flops 1019215872 | bytes 4580352 | tf_op jit(solution)/shard_map/pallas_call | solution.py:160
  37.8 2.1 %shard_map.111.refs_2_ = bf16[3,8,80,256]{3,2,1,0:T(8,128)(2,1)S(1)} custom-call(s32[3]{0:T(128)S(1)} %pad_add_fusion.info, bf16[576,256]{1,0:T(8,128)(2,1)S(1)} %get-tuple-element.94.refs_0_.refs_4_, bf16[576,256]{1,0:T(8,128)(2,1)S(1)} %collective-permute-done.3.refs_1_.refs_4_.refs_8_.refs_12_.refs_16_, ...), custom_call_target="tpu_custom_call" | custom-call | flops 1019215872 | bytes 4580352 | tf_op jit(solution)/shard_map/pallas_call | solution.py:160
  39.9 2.1 %shard_map.112.refs_3_ = bf16[3,8,80,256]{3,2,1,0:T(8,128)(2,1)S(1)} custom-call(s32[3]{0:T(128)S(1)} %pad_add_fusion.info, bf16[576,256]{1,0:T(8,128)(2,1)S(1)} %get-tuple-element.93.refs_0_.refs_5_, bf16[576,256]{1,0:T(8,128)(2,1)S(1)} %collective-permute-done.4.refs_1_.refs_5_.refs_9_.refs_13_.refs_17_, ...), custom_call_target="tpu_custom_call" | custom-call | flops 1019215872 | bytes 4580352 | tf_op jit(solution)/shard_map/pallas_call | solution.py:160
  42.1 6.8 %shard_map.114 = bf16[576,512]{1,0:T(8,128)(2,1)S(1)} custom-call(s32[3]{0:T(128)S(1)} %pad_add_fusion.info, bf16[3,8,80,256]{3,2,1,0:T(8,128)(2,1)S(1)} %get-tuple-element.49.refs_0_, bf16[3,8,80,256]{3,2,1,0:T(8,128)(2,1)S(1)} %shard_map.110.refs_1_, bf16[3,8,80,256]{3,2,1,0:T(8,128)(2,1)S(1)} %shard_map.111.refs_2_, ...), custom_call_target="tpu_custom_call" | custom-call | flops 4831838208 | bytes 4259840 | tf_op jit(solution)/shard_map/pallas_call | solution.py:160
  48.9 1.7 %collective-permute-start.5 = (bf16[576,512]{1,0:T(8,128)(2,1)S(1)}, bf16[576,512]{1,0:T(8,128)(2,1)S(1)}, u32[]{:S(2)}, u32[]{:S(2)}) collective-permute-start(bf16[576,512]{1,0:T(8,128)(2,1)S(1)} %shard_map.114), channel_id=1, source_target_pairs={{0,2},{2,0},{1,3},{3,1},{4,6},{6,4},{5,7},{7,5},{8,10},{10,8},{9,1... | collective-permute-start | bytes 1769480 | tf_op jit(solution)/shard_map/ppermute | solution.py:514
  51.0 1.7 %collective-permute-start.16 = (bf16[144,1152]{1,0:T(8,128)(2,1)S(1)}, bf16[144,1152]{1,0:T(8,128)(2,1)S(1)}, u32[]{:S(2)}, u32[]{:S(2)}) collective-permute-start(bf16[144,1152]{1,0:T(8,128)(2,1)S(1)} %get-tuple-element.68), channel_id=1, source_target_pairs={{0,2},{2,0},{1,3},{3,1},{4,6},{6,4},{5,7},{7,5},{8,10},{10,8},{9,1... | collective-permute-start | bytes 995336 | tf_op jit(solution)/shard_map/ppermute | solution.py:514
  52.7 19.5 %collective-permute-done.9.refs_18_ = bf16[144,1152]{1,0:T(8,128)(2,1)S(1)} collective-permute-done((bf16[144,1152]{1,0:T(8,128)(2,1)S(1)}, bf16[144,1152]{1,0:T(8,128)(2,1)S(1)}, u32[]{:S(2)}, u32[]{:S(2)}) %collective-permute-start.9) | collective-permute-done | bytes 331808 | tf_op jit(solution)/shard_map/ppermute | solution.py:514
  72.2 1.7 collective-permute-start.11
  73.9 6.8 %shard_map.113.refs_0_ = bf16[576,512]{1,0:T(8,128)(2,1)S(1)} custom-call(s32[3]{0:T(128)S(1)} %pad_add_fusion.info, bf16[3,8,80,256]{3,2,1,0:T(8,128)(2,1)S(1)} %get-tuple-element.49.refs_0_, bf16[3,8,80,256]{3,2,1,0:T(8,128)(2,1)S(1)} %shard_map.110.refs_1_, bf16[3,8,80,256]{3,2,1,0:T(8,128)(2,1)S(1)} %shard_map.111.refs_2_, ...), custom_call_target="tpu_custom_call" | custom-call | flops 4831838208 | bytes 4259840 | tf_op jit(solution)/shard_map/pallas_call | solution.py:160
  81.3 2.2 %shard_map.115 = (bf16[592,128]{1,0:T(8,128)(2,1)S(1)}, bf16[592,128]{1,0:T(8,128)(2,1)S(1)}, bf16[592,128]{1,0:T(8,128)(2,1)S(1)}, bf16[592,128]{1,0:T(8,128)(2,1)S(1)}) custom-call(s32[3]{0:T(128)S(1)} %pad_add_fusion.info, bf16[576,512]{1,0:T(8,128)(2,1)S(1)} %shard_map.113.refs_0_, bf16[576,512]{1,0:T(8,128)(2,1)S(1)} %collective-permute-done.5.refs_1_, ...), custom_call_target="tpu_custom_call" | custom-call | flops 679477248 | bytes 3686400 | tf_op jit(solution)/shard_map/pallas_call | solution.py:160
  83.4 1.6 collective-permute-start.28
  85.5 1.5 collective-permute-start.18
  87.6 1.8 %shard_map.117 = (bf16[576,128]{1,0:T(8,128)(2,1)S(1)}, bf16[576,128]{1,0:T(8,128)(2,1)S(1)}, bf16[576,128]{1,0:T(8,128)(2,1)S(1)}, bf16[576,128]{1,0:T(8,128)(2,1)S(1)}) custom-call(s32[3]{0:T(128)S(1)} %pad_add_fusion.info, bf16[576,512]{1,0:T(8,128)(2,1)S(1)} %shard_map.113.refs_0_, bf16[576,512]{1,0:T(8,128)(2,1)S(1)} %collective-permute-done.5.refs_1_, ...), custom_call_target="tpu_custom_call" | custom-call | flops 679477248 | bytes 7225344 | tf_op jit(solution)/shard_map/pallas_call | solution.py:160
  89.3 4.8 %collective-permute-done.28.refs_23_ = bf16[144,1152]{1,0:T(8,128)(2,1)S(1)} collective-permute-done((bf16[144,1152]{1,0:T(8,128)(2,1)S(1)}, bf16[144,1152]{1,0:T(8,128)(2,1)S(1)}, u32[]{:S(2)}, u32[]{:S(2)}) %collective-permute-start.28) | collective-permute-done | bytes 331808 | tf_op jit(solution)/shard_map/ppermute | solution.py:514
  94.5 1.7 %collective-permute-start.6 = (bf16[592,128]{1,0:T(8,128)(2,1)S(1)}, bf16[592,128]{1,0:T(8,128)(2,1)S(1)}, u32[]{:S(2)}, u32[]{:S(2)}) collective-permute-start(bf16[592,128]{1,0:T(8,128)(2,1)S(1)} %get-tuple-element.55), channel_id=1, source_target_pairs={{0,4},{4,8},{8,12},{12,0},{1,5},{5,9},{9,13},{13,1},{2,6},{6,10},{... | collective-permute-start | bytes 454664 | tf_op jit(solution)/shard_map/ppermute | solution.py:514
  96.3 5.0 %collective-permute-done.17.refs_12_ = bf16[144,1152]{1,0:T(8,128)(2,1)S(1)} collective-permute-done((bf16[144,1152]{1,0:T(8,128)(2,1)S(1)}, bf16[144,1152]{1,0:T(8,128)(2,1)S(1)}, u32[]{:S(2)}, u32[]{:S(2)}) %collective-permute-start.17) | collective-permute-done | bytes 331808 | tf_op jit(solution)/shard_map/ppermute | solution.py:514
  101.3 2.6 %collective-permute-start.7 = (bf16[592,128]{1,0:T(8,128)(2,1)S(1)}, bf16[592,128]{1,0:T(8,128)(2,1)S(1)}, u32[]{:S(2)}, u32[]{:S(2)}) collective-permute-start(bf16[592,128]{1,0:T(8,128)(2,1)S(1)} %get-tuple-element.56), channel_id=1, source_target_pairs={{0,8},{4,12},{8,0},{12,4},{1,9},{5,13},{9,1},{13,5},{2,10},{6,14},... | collective-permute-start | bytes 454664 | tf_op jit(solution)/shard_map/ppermute | solution.py:514
  103.9 3.6 %collective-permute-done.18.refs_13_ = bf16[144,1152]{1,0:T(8,128)(2,1)S(1)} collective-permute-done((bf16[144,1152]{1,0:T(8,128)(2,1)S(1)}, bf16[144,1152]{1,0:T(8,128)(2,1)S(1)}, u32[]{:S(2)}, u32[]{:S(2)}) %collective-permute-start.18) | collective-permute-done | bytes 331808 | tf_op jit(solution)/shard_map/ppermute | solution.py:514
  107.5 3.6 %collective-permute-start.8 = (bf16[592,128]{1,0:T(8,128)(2,1)S(1)}, bf16[592,128]{1,0:T(8,128)(2,1)S(1)}, u32[]{:S(2)}, u32[]{:S(2)}) collective-permute-start(bf16[592,128]{1,0:T(8,128)(2,1)S(1)} %get-tuple-element.57), channel_id=1, source_target_pairs={{0,12},{4,0},{8,4},{12,8},{1,13},{5,1},{9,5},{13,9},{2,14},{6,2},{... | collective-permute-start | bytes 454664 | tf_op jit(solution)/shard_map/ppermute | solution.py:514
  111.6 1.5 collective-permute-start.24
  113.1 2.2 %collective-permute-done.8.refs_3_ = bf16[592,128]{1,0:T(8,128)(2,1)S(1)} collective-permute-done((bf16[592,128]{1,0:T(8,128)(2,1)S(1)}, bf16[592,128]{1,0:T(8,128)(2,1)S(1)}, u32[]{:S(2)}, u32[]{:S(2)}) %collective-permute-start.8) | collective-permute-done | bytes 151584 | tf_op jit(solution)/shard_map/ppermute | solution.py:514
  115.3 4.8 %collective-permute-done.13.refs_5_ = bf16[576,128]{1,0:T(8,128)(2,1)S(1)} collective-permute-done((bf16[576,128]{1,0:T(8,128)(2,1)S(1)}, bf16[576,128]{1,0:T(8,128)(2,1)S(1)}, u32[]{:S(2)}, u32[]{:S(2)}) %collective-permute-start.13) | collective-permute-done | bytes 147488 | tf_op jit(solution)/shard_map/ppermute | solution.py:514
  120.6 1.2 collective-permute-done.23.refs_18_
  121.8 5.1 %collective-permute-done.24.refs_19_ = bf16[144,1152]{1,0:T(8,128)(2,1)S(1)} collective-permute-done((bf16[144,1152]{1,0:T(8,128)(2,1)S(1)}, bf16[144,1152]{1,0:T(8,128)(2,1)S(1)}, u32[]{:S(2)}, u32[]{:S(2)}) %collective-permute-start.24) | collective-permute-done | bytes 331808 | tf_op jit(solution)/shard_map/ppermute | solution.py:514
  127.3 2.1 %collective-permute-done.14.refs_6_ = bf16[576,128]{1,0:T(8,128)(2,1)S(1)} collective-permute-done((bf16[576,128]{1,0:T(8,128)(2,1)S(1)}, bf16[576,128]{1,0:T(8,128)(2,1)S(1)}, u32[]{:S(2)}, u32[]{:S(2)}) %collective-permute-start.14) | collective-permute-done | bytes 147488 | tf_op jit(solution)/shard_map/ppermute | solution.py:514
  129.4 3.0 %collective-permute-done.15.refs_7_ = bf16[576,128]{1,0:T(8,128)(2,1)S(1)} collective-permute-done((bf16[576,128]{1,0:T(8,128)(2,1)S(1)}, bf16[576,128]{1,0:T(8,128)(2,1)S(1)}, u32[]{:S(2)}, u32[]{:S(2)}) %collective-permute-start.15) | collective-permute-done | bytes 147488 | tf_op jit(solution)/shard_map/ppermute | solution.py:514
  133.4 0.6 collective-permute-done.21.refs_16_
  135.4 9.1 %shard_map.118 = (bf16[4,2,288,128]{3,2,1,0:T(8,128)(2,1)S(1)}, bf16[4,2,288,128]{3,2,1,0:T(8,128)(2,1)S(1)}, f32[4,128]{1,0:T(4,128)S(1)}) custom-call(s32[3]{0:T(128)S(1)} %pad_add_fusion.info, bf16[592,128]{1,0:T(8,128)(2,1)S(1)} %get-tuple-element.54.refs_0_, bf16[592,128]{1,0:T(8,128)(2,1)S(1)} %collective-permute-done.6.refs_1_, ...), custom_call_target="tpu_custom_call" | custom-call | flops 5435817984 | bytes 11822080 | tf_op jit(solution)/shard_map/pallas_call | solution.py:160
  144.7 1.9 %collective-permute-done.32.other = bf16[4,2,288,128]{3,2,1,0:T(8,128)(2,1)S(1)} collective-permute-done((bf16[4,2,288,128]{3,2,1,0:T(8,128)(2,1)S(1)}, bf16[4,2,288,128]{3,2,1,0:T(8,128)(2,1)S(1)}, u32[]{:S(2)}, u32[]{:S(2)}) %collective-permute-start.32) | collective-permute-done | bytes 589856 | tf_op jit(solution)/shard_map/ppermute | solution.py:514
  146.6 0.8 shard_map.119
  147.5 1.6 collective-permute-start.33
  149.0 2.8 %collective-permute-start.34 = (bf16[288,128]{1,0:T(8,128)(2,1)S(1)}, bf16[288,128]{1,0:T(8,128)(2,1)S(1)}, u32[]{:S(2)}, u32[]{:S(2)}) collective-permute-start(bf16[288,128]{1,0:T(8,128)(2,1)S(1)} %get-tuple-element.87), channel_id=1, source_target_pairs={{0,12},{2,14},{4,0},{6,2},{8,4},{10,6},{12,8},{14,10},{1,13},{3,15... | collective-permute-start | bytes 221192 | tf_op jit(solution)/shard_map/ppermute | solution.py:691
  151.8 0.7 collective-permute-start.36
  152.5 3.1 %collective-permute-start.37 = (bf16[288,128]{1,0:T(8,128)(2,1)S(1)}, bf16[288,128]{1,0:T(8,128)(2,1)S(1)}, u32[]{:S(2)}, u32[]{:S(2)}) collective-permute-start(bf16[288,128]{1,0:T(8,128)(2,1)S(1)} %get-tuple-element.90), channel_id=1, source_target_pairs={{0,10},{2,8},{4,14},{6,12},{8,2},{10,0},{12,6},{14,4},{1,11},{3,9}... | collective-permute-start | bytes 221192 | tf_op jit(solution)/shard_map/ppermute | solution.py:691
  155.6 2.0 %collective-permute-start.38 = (bf16[288,128]{1,0:T(8,128)(2,1)S(1)}, bf16[288,128]{1,0:T(8,128)(2,1)S(1)}, u32[]{:S(2)}, u32[]{:S(2)}) collective-permute-start(bf16[288,128]{1,0:T(8,128)(2,1)S(1)} %get-tuple-element.91), channel_id=1, source_target_pairs={{0,4},{2,6},{4,8},{6,10},{8,12},{10,14},{12,0},{14,2},{1,5},{3,7},... | collective-permute-start | bytes 221192 | tf_op jit(solution)/shard_map/ppermute | solution.py:691
  157.8 5.2 %collective-permute-done.36.refs_4_ = bf16[288,128]{1,0:T(8,128)(2,1)S(1)} collective-permute-done((bf16[288,128]{1,0:T(8,128)(2,1)S(1)}, bf16[288,128]{1,0:T(8,128)(2,1)S(1)}, u32[]{:S(2)}, u32[]{:S(2)}) %collective-permute-start.36) | collective-permute-done | bytes 73760 | tf_op jit(solution)/shard_map/ppermute | solution.py:691
  163.0 2.2 %collective-permute-done.37.refs_5_ = bf16[288,128]{1,0:T(8,128)(2,1)S(1)} collective-permute-done((bf16[288,128]{1,0:T(8,128)(2,1)S(1)}, bf16[288,128]{1,0:T(8,128)(2,1)S(1)}, u32[]{:S(2)}, u32[]{:S(2)}) %collective-permute-start.37) | collective-permute-done | bytes 73760 | tf_op jit(solution)/shard_map/ppermute | solution.py:691
  165.2 1.5 shard_map.120
  (70 shorter events, 7.4 us)
Async XLA Ops:
  0.0 9.1 %copy-start.7 = (bf16[1152]{0:T(1024)(128)(2,1)S(1)}, bf16[1152]{0:T(1024)(128)(2,1)}, u32[]{:S(2)}) copy-start(bf16[1152]{0:T(1024)(128)(2,1)} %param.16) | copy-start | bytes 6916
  0.0 9.1 %copy-start.8 = (bf16[1152]{0:T(1024)(128)(2,1)S(1)}, bf16[1152]{0:T(1024)(128)(2,1)}, u32[]{:S(2)}) copy-start(bf16[1152]{0:T(1024)(128)(2,1)} %param.19) | copy-start | bytes 6916
  0.0 17.2 %collective-permute-start = (bf16[576,128]{1,0:T(8,128)(2,1)}, bf16[576,128]{1,0:T(8,128)(2,1)S(1)}, u32[]{:S(2)}, u32[]{:S(2)}) collective-permute-start(bf16[576,128]{1,0:T(8,128)(2,1)} %bitcast.11), channel_id=1, source_target_pairs={{0,2},{2,0},{1,3},{3,1},{4,6},{6,4},{5,7},{7,5},{8,10},{10,8},{9,1... | collective-permute-start | bytes 442376 | tf_op jit(solution)/shard_map/ppermute | solution.py:514
  5.0 8.4 %copy-start.1 = (bf16[576,1152]{1,0:T(8,128)(2,1)S(1)}, bf16[576,1152]{1,0:T(8,128)(2,1)}, u32[]{:S(2)}) copy-start(bf16[576,1152]{1,0:T(8,128)(2,1)} %refs_0_.1) | copy-start | bytes 3981316
  5.0 34.9 %collective-permute-start.4 = (bf16[576,256]{1,0:T(8,128)(2,1)S(1)}, bf16[576,256]{1,0:T(8,128)(2,1)S(1)}, u32[]{:S(2)}, u32[]{:S(2)}) collective-permute-start(bf16[576,256]{1,0:T(8,128)(2,1)S(1)} %get-tuple-element.93.refs_0_.refs_5_), channel_id=1, source_target_pairs={{0,2},{2,0},{1,3},{3,1},{4,6},{6,4},{5,7},{7,5},{8,10},{10,8},{9,1... | collective-permute-start | bytes 884744 | tf_op jit(solution)/shard_map/ppermute | solution.py:514
  5.0 32.8 %collective-permute-start.3 = (bf16[576,256]{1,0:T(8,128)(2,1)S(1)}, bf16[576,256]{1,0:T(8,128)(2,1)S(1)}, u32[]{:S(2)}, u32[]{:S(2)}) collective-permute-start(bf16[576,256]{1,0:T(8,128)(2,1)S(1)} %get-tuple-element.94.refs_0_.refs_4_), channel_id=1, source_target_pairs={{0,2},{2,0},{1,3},{3,1},{4,6},{6,4},{5,7},{7,5},{8,10},{10,8},{9,1... | collective-permute-start | bytes 884744 | tf_op jit(solution)/shard_map/ppermute | solution.py:514
  7.0 28.2 %collective-permute-start.2 = (bf16[576,256]{1,0:T(8,128)(2,1)}, bf16[576,256]{1,0:T(8,128)(2,1)S(1)}, u32[]{:S(2)}, u32[]{:S(2)}) collective-permute-start(bf16[576,256]{1,0:T(8,128)(2,1)} %get-tuple-element.95.refs_0_.refs_3_), channel_id=1, source_target_pairs={{0,2},{2,0},{1,3},{3,1},{4,6},{6,4},{5,7},{7,5},{8,10},{10,8},{9,1... | collective-permute-start | bytes 884744 | tf_op jit(solution)/shard_map/ppermute | solution.py:514
  7.0 25.4 %collective-permute-start.1 = (bf16[576,256]{1,0:T(8,128)(2,1)S(1)}, bf16[576,256]{1,0:T(8,128)(2,1)S(1)}, u32[]{:S(2)}, u32[]{:S(2)}) collective-permute-start(bf16[576,256]{1,0:T(8,128)(2,1)S(1)} %get-tuple-element.96.refs_2_), channel_id=1, source_target_pairs={{0,2},{2,0},{1,3},{3,1},{4,6},{6,4},{5,7},{7,5},{8,10},{10,8},{9,1... | collective-permute-start | bytes 884744 | tf_op jit(solution)/shard_map/ppermute | solution.py:514
  13.4 2.1 %copy-start.2 = (bf16[3,576,1152]{2,1,0:T(8,128)(2,1)S(1)}, bf16[3,576,1152]{2,1,0:T(8,128)(2,1)}, u32[]{:S(2)}) copy-start(bf16[3,576,1152]{2,1,0:T(8,128)(2,1)} %refs_9_.1) | copy-start | bytes 11943940
  16.8 15.6 %copy-start = (bf16[3,576,1152]{2,1,0:T(8,128)(2,1)S(1)}, bf16[3,576,1152]{2,1,0:T(8,128)(2,1)}, u32[]{:S(2)}) copy-start(bf16[3,576,1152]{2,1,0:T(8,128)(2,1)} %refs_3_.5) | copy-start | bytes 11943940
  16.8 15.6 %copy-start.6 = (bf16[1,1,576,128]{3,2,1,0:T(8,128)(2,1)S(1)}, bf16[1,1,576,128]{3,2,1,0:T(8,128)(2,1)}, u32[]{:S(2)}) copy-start(bf16[1,1,576,128]{3,2,1,0:T(8,128)(2,1)} %param.12) | copy-start | bytes 442372
  48.9 32.4 %collective-permute-start.5 = (bf16[576,512]{1,0:T(8,128)(2,1)S(1)}, bf16[576,512]{1,0:T(8,128)(2,1)S(1)}, u32[]{:S(2)}, u32[]{:S(2)}) collective-permute-start(bf16[576,512]{1,0:T(8,128)(2,1)S(1)} %shard_map.114), channel_id=1, source_target_pairs={{0,2},{2,0},{1,3},{3,1},{4,6},{6,4},{5,7},{7,5},{8,10},{10,8},{9,1... | collective-permute-start | bytes 1769480 | tf_op jit(solution)/shard_map/ppermute | solution.py:514
  50.5 21.7 %collective-permute-start.9 = (bf16[144,1152]{1,0:T(8,128)(2,1)S(1)}, bf16[144,1152]{1,0:T(8,128)(2,1)S(1)}, u32[]{:S(2)}, u32[]{:S(2)}) collective-permute-start(bf16[144,1152]{1,0:T(8,128)(2,1)S(1)} %get-tuple-element.59), channel_id=1, source_target_pairs={{0,2},{2,0},{1,3},{3,1},{4,6},{6,4},{5,7},{7,5},{8,10},{10,8},{9,1... | collective-permute-start | bytes 995336 | tf_op jit(solution)/shard_map/ppermute | solution.py:514
  51.0 34.5 %collective-permute-start.16 = (bf16[144,1152]{1,0:T(8,128)(2,1)S(1)}, bf16[144,1152]{1,0:T(8,128)(2,1)S(1)}, u32[]{:S(2)}, u32[]{:S(2)}) collective-permute-start(bf16[144,1152]{1,0:T(8,128)(2,1)S(1)} %get-tuple-element.68), channel_id=1, source_target_pairs={{0,2},{2,0},{1,3},{3,1},{4,6},{6,4},{5,7},{7,5},{8,10},{10,8},{9,1... | collective-permute-start | bytes 995336 | tf_op jit(solution)/shard_map/ppermute | solution.py:514
  72.2 8.5 %collective-permute-start.11 = (bf16[144,1152]{1,0:T(8,128)(2,1)S(1)}, bf16[144,1152]{1,0:T(8,128)(2,1)S(1)}, u32[]{:S(2)}, u32[]{:S(2)}) collective-permute-start(bf16[144,1152]{1,0:T(8,128)(2,1)S(1)} %collective-permute-done.9.refs_18_), channel_id=1, source_target_pairs={{0,16},{16,0},{1,17},{17,1},{2,18},{18,2},{3,19},{19,3},{4,20},{20... | collective-permute-start | bytes 995336 | tf_op jit(solution)/shard_map/ppermute | solution.py:514
  80.7 6.3 %collective-permute-start.10 = (bf16[144,1152]{1,0:T(8,128)(2,1)S(1)}, bf16[144,1152]{1,0:T(8,128)(2,1)S(1)}, u32[]{:S(2)}, u32[]{:S(2)}) collective-permute-start(bf16[144,1152]{1,0:T(8,128)(2,1)S(1)} %collective-permute-done.9.refs_18_), channel_id=1, source_target_pairs={{0,1},{1,0},{2,3},{3,2},{4,5},{5,4},{6,7},{7,6},{8,9},{9,8},{10,11... | collective-permute-start | bytes 995336 | tf_op jit(solution)/shard_map/ppermute | solution.py:514
  80.8 6.8 %collective-permute-start.12 = (bf16[144,1152]{1,0:T(8,128)(2,1)S(1)}, bf16[144,1152]{1,0:T(8,128)(2,1)S(1)}, u32[]{:S(2)}, u32[]{:S(2)}) collective-permute-start(bf16[144,1152]{1,0:T(8,128)(2,1)S(1)} %collective-permute-done.11.refs_20_), channel_id=1, source_target_pairs={{0,1},{1,0},{2,3},{3,2},{4,5},{5,4},{6,7},{7,6},{8,9},{9,8},{10,11... | collective-permute-start | bytes 995336 | tf_op jit(solution)/shard_map/ppermute | solution.py:514
  83.4 10.7 %collective-permute-start.28 = (bf16[144,1152]{1,0:T(8,128)(2,1)S(1)}, bf16[144,1152]{1,0:T(8,128)(2,1)S(1)}, u32[]{:S(2)}, u32[]{:S(2)}) collective-permute-start(bf16[144,1152]{1,0:T(8,128)(2,1)S(1)} %get-tuple-element.79), channel_id=1, source_target_pairs={{0,2},{2,0},{1,3},{3,1},{4,6},{6,4},{5,7},{7,5},{8,10},{10,8},{9,1... | collective-permute-start | bytes 995336 | tf_op jit(solution)/shard_map/ppermute | solution.py:514
  85.0 16.3 %collective-permute-start.17 = (bf16[144,1152]{1,0:T(8,128)(2,1)S(1)}, bf16[144,1152]{1,0:T(8,128)(2,1)S(1)}, u32[]{:S(2)}, u32[]{:S(2)}) collective-permute-start(bf16[144,1152]{1,0:T(8,128)(2,1)S(1)} %get-tuple-element.69), channel_id=1, source_target_pairs={{0,2},{2,0},{1,3},{3,1},{4,6},{6,4},{5,7},{7,5},{8,10},{10,8},{9,1... | collective-permute-start | bytes 995336 | tf_op jit(solution)/shard_map/ppermute | solution.py:514
  85.5 49.9 %copy-start.3 = (bf16[3,576,1152]{2,1,0:T(8,128)(2,1)S(1)}, bf16[3,576,1152]{2,1,0:T(8,128)(2,1)}, u32[]{:S(2)}) copy-start(bf16[3,576,1152]{2,1,0:T(8,128)(2,1)} %refs_9_.1) | copy-start | bytes 11943940
  85.5 49.9 %copy-start.5 = (bf16[576,1152]{1,0:T(8,128)(2,1)S(1)}, bf16[576,1152]{1,0:T(8,128)(2,1)}, u32[]{:S(2)}) copy-start(bf16[576,1152]{1,0:T(8,128)(2,1)} %refs_10_.1) | copy-start | bytes 3981316
  85.5 22.0 %collective-permute-start.18 = (bf16[144,1152]{1,0:T(8,128)(2,1)S(1)}, bf16[144,1152]{1,0:T(8,128)(2,1)S(1)}, u32[]{:S(2)}, u32[]{:S(2)}) collective-permute-start(bf16[144,1152]{1,0:T(8,128)(2,1)S(1)} %get-tuple-element.70), channel_id=1, source_target_pairs={{0,2},{2,0},{1,3},{3,1},{4,6},{6,4},{5,7},{7,5},{8,10},{10,8},{9,1... | collective-permute-start | bytes 995336 | tf_op jit(solution)/shard_map/ppermute | solution.py:514
  87.0 24.1 %collective-permute-start.22 = (bf16[144,1152]{1,0:T(8,128)(2,1)S(1)}, bf16[144,1152]{1,0:T(8,128)(2,1)S(1)}, u32[]{:S(2)}, u32[]{:S(2)}) collective-permute-start(bf16[144,1152]{1,0:T(8,128)(2,1)S(1)} %collective-permute-done.16.refs_11_), channel_id=1, source_target_pairs={{0,16},{16,0},{1,17},{17,1},{2,18},{18,2},{3,19},{19,3},{4,20},{20... | collective-permute-start | bytes 995336 | tf_op jit(solution)/shard_map/ppermute | solution.py:514
  94.2 25.9 %collective-permute-start.30 = (bf16[144,1152]{1,0:T(8,128)(2,1)S(1)}, bf16[144,1152]{1,0:T(8,128)(2,1)S(1)}, u32[]{:S(2)}, u32[]{:S(2)}) collective-permute-start(bf16[144,1152]{1,0:T(8,128)(2,1)S(1)} %collective-permute-done.28.refs_23_), channel_id=1, source_target_pairs={{0,16},{16,0},{1,17},{17,1},{2,18},{18,2},{3,19},{19,3},{4,20},{20... | collective-permute-start | bytes 995336 | tf_op jit(solution)/shard_map/ppermute | solution.py:514
  94.5 17.1 %collective-permute-start.6 = (bf16[592,128]{1,0:T(8,128)(2,1)S(1)}, bf16[592,128]{1,0:T(8,128)(2,1)S(1)}, u32[]{:S(2)}, u32[]{:S(2)}) collective-permute-start(bf16[592,128]{1,0:T(8,128)(2,1)S(1)} %get-tuple-element.55), channel_id=1, source_target_pairs={{0,4},{4,8},{8,12},{12,0},{1,5},{5,9},{9,13},{13,1},{2,6},{6,10},{... | collective-permute-start | bytes 454664 | tf_op jit(solution)/shard_map/ppermute | solution.py:514
  101.3 11.9 %collective-permute-start.7 = (bf16[592,128]{1,0:T(8,128)(2,1)S(1)}, bf16[592,128]{1,0:T(8,128)(2,1)S(1)}, u32[]{:S(2)}, u32[]{:S(2)}) collective-permute-start(bf16[592,128]{1,0:T(8,128)(2,1)S(1)} %get-tuple-element.56), channel_id=1, source_target_pairs={{0,8},{4,12},{8,0},{12,4},{1,9},{5,13},{9,1},{13,5},{2,10},{6,14},... | collective-permute-start | bytes 454664 | tf_op jit(solution)/shard_map/ppermute | solution.py:514
  107.5 7.8 %collective-permute-start.8 = (bf16[592,128]{1,0:T(8,128)(2,1)S(1)}, bf16[592,128]{1,0:T(8,128)(2,1)S(1)}, u32[]{:S(2)}, u32[]{:S(2)}) collective-permute-start(bf16[592,128]{1,0:T(8,128)(2,1)S(1)} %get-tuple-element.57), channel_id=1, source_target_pairs={{0,12},{4,0},{8,4},{12,8},{1,13},{5,1},{9,5},{13,9},{2,14},{6,2},{... | collective-permute-start | bytes 454664 | tf_op jit(solution)/shard_map/ppermute | solution.py:514
  111.1 10.7 %collective-permute-start.23 = (bf16[144,1152]{1,0:T(8,128)(2,1)S(1)}, bf16[144,1152]{1,0:T(8,128)(2,1)S(1)}, u32[]{:S(2)}, u32[]{:S(2)}) collective-permute-start(bf16[144,1152]{1,0:T(8,128)(2,1)S(1)} %collective-permute-done.17.refs_12_), channel_id=1, source_target_pairs={{0,16},{16,0},{1,17},{17,1},{2,18},{18,2},{3,19},{19,3},{4,20},{20... | collective-permute-start | bytes 995336 | tf_op jit(solution)/shard_map/ppermute | solution.py:514
  111.6 15.2 %collective-permute-start.24 = (bf16[144,1152]{1,0:T(8,128)(2,1)S(1)}, bf16[144,1152]{1,0:T(8,128)(2,1)S(1)}, u32[]{:S(2)}, u32[]{:S(2)}) collective-permute-start(bf16[144,1152]{1,0:T(8,128)(2,1)S(1)} %collective-permute-done.18.refs_13_), channel_id=1, source_target_pairs={{0,16},{16,0},{1,17},{17,1},{2,18},{18,2},{3,19},{19,3},{4,20},{20... | collective-permute-start | bytes 995336 | tf_op jit(solution)/shard_map/ppermute | solution.py:514
  113.1 6.9 %collective-permute-start.13 = (bf16[576,128]{1,0:T(8,128)(2,1)S(1)}, bf16[576,128]{1,0:T(8,128)(2,1)S(1)}, u32[]{:S(2)}, u32[]{:S(2)}) collective-permute-start(bf16[576,128]{1,0:T(8,128)(2,1)S(1)} %get-tuple-element.64), channel_id=1, source_target_pairs={{0,4},{4,8},{8,12},{12,0},{1,5},{5,9},{9,13},{13,1},{2,6},{6,10},{... | collective-permute-start | bytes 442376 | tf_op jit(solution)/shard_map/ppermute | solution.py:514
  115.3 17.1 %collective-permute-start.29 = (bf16[144,1152]{1,0:T(8,128)(2,1)S(1)}, bf16[144,1152]{1,0:T(8,128)(2,1)S(1)}, u32[]{:S(2)}, u32[]{:S(2)}) collective-permute-start(bf16[144,1152]{1,0:T(8,128)(2,1)S(1)} %collective-permute-done.28.refs_23_), channel_id=1, source_target_pairs={{0,1},{1,0},{2,3},{3,2},{4,5},{5,4},{6,7},{7,6},{8,9},{9,8},{10,11... | collective-permute-start | bytes 995336 | tf_op jit(solution)/shard_map/ppermute | solution.py:514
  120.1 12.8 %collective-permute-start.19 = (bf16[144,1152]{1,0:T(8,128)(2,1)S(1)}, bf16[144,1152]{1,0:T(8,128)(2,1)S(1)}, u32[]{:S(2)}, u32[]{:S(2)}) collective-permute-start(bf16[144,1152]{1,0:T(8,128)(2,1)S(1)} %collective-permute-done.16.refs_11_), channel_id=1, source_target_pairs={{0,1},{1,0},{2,3},{3,2},{4,5},{5,4},{6,7},{7,6},{8,9},{9,8},{10,11... | collective-permute-start | bytes 995336 | tf_op jit(solution)/shard_map/ppermute | solution.py:514
  120.1 12.9 %collective-permute-start.25 = (bf16[144,1152]{1,0:T(8,128)(2,1)S(1)}, bf16[144,1152]{1,0:T(8,128)(2,1)S(1)}, u32[]{:S(2)}, u32[]{:S(2)}) collective-permute-start(bf16[144,1152]{1,0:T(8,128)(2,1)S(1)} %collective-permute-done.22.refs_17_), channel_id=1, source_target_pairs={{0,1},{1,0},{2,3},{3,2},{4,5},{5,4},{6,7},{7,6},{8,9},{9,8},{10,11... | collective-permute-start | bytes 995336 | tf_op jit(solution)/shard_map/ppermute | solution.py:514
  121.8 7.6 %collective-permute-start.14 = (bf16[576,128]{1,0:T(8,128)(2,1)S(1)}, bf16[576,128]{1,0:T(8,128)(2,1)S(1)}, u32[]{:S(2)}, u32[]{:S(2)}) collective-permute-start(bf16[576,128]{1,0:T(8,128)(2,1)S(1)} %get-tuple-element.65), channel_id=1, source_target_pairs={{0,8},{4,12},{8,0},{12,4},{1,9},{5,13},{9,1},{13,5},{2,10},{6,14},... | collective-permute-start | bytes 442376 | tf_op jit(solution)/shard_map/ppermute | solution.py:514
  126.9 5.5 %collective-permute-start.15 = (bf16[576,128]{1,0:T(8,128)(2,1)S(1)}, bf16[576,128]{1,0:T(8,128)(2,1)S(1)}, u32[]{:S(2)}, u32[]{:S(2)}) collective-permute-start(bf16[576,128]{1,0:T(8,128)(2,1)S(1)} %get-tuple-element.66), channel_id=1, source_target_pairs={{0,12},{4,0},{8,4},{12,8},{1,13},{5,1},{9,5},{13,9},{2,14},{6,2},{... | collective-permute-start | bytes 442376 | tf_op jit(solution)/shard_map/ppermute | solution.py:514
  129.4 4.0 %collective-permute-start.20 = (bf16[144,1152]{1,0:T(8,128)(2,1)S(1)}, bf16[144,1152]{1,0:T(8,128)(2,1)S(1)}, u32[]{:S(2)}, u32[]{:S(2)}) collective-permute-start(bf16[144,1152]{1,0:T(8,128)(2,1)S(1)} %collective-permute-done.17.refs_12_), channel_id=1, source_target_pairs={{0,1},{1,0},{2,3},{3,2},{4,5},{5,4},{6,7},{7,6},{8,9},{9,8},{10,11... | collective-permute-start | bytes 995336 | tf_op jit(solution)/shard_map/ppermute | solution.py:514
  132.4 1.6 collective-permute-start.21
  132.4 2.1 %collective-permute-start.31 = (bf16[144,1152]{1,0:T(8,128)(2,1)S(1)}, bf16[144,1152]{1,0:T(8,128)(2,1)S(1)}, u32[]{:S(2)}, u32[]{:S(2)}) collective-permute-start(bf16[144,1152]{1,0:T(8,128)(2,1)S(1)} %collective-permute-done.30.refs_25_), channel_id=1, source_target_pairs={{0,1},{1,0},{2,3},{3,2},{4,5},{5,4},{6,7},{7,6},{8,9},{9,8},{10,11... | collective-permute-start | bytes 995336 | tf_op jit(solution)/shard_map/ppermute | solution.py:514
  132.9 2.1 %collective-permute-start.26 = (bf16[144,1152]{1,0:T(8,128)(2,1)S(1)}, bf16[144,1152]{1,0:T(8,128)(2,1)S(1)}, u32[]{:S(2)}, u32[]{:S(2)}) collective-permute-start(bf16[144,1152]{1,0:T(8,128)(2,1)S(1)} %collective-permute-done.23.refs_18_), channel_id=1, source_target_pairs={{0,1},{1,0},{2,3},{3,2},{4,5},{5,4},{6,7},{7,6},{8,9},{9,8},{10,11... | collective-permute-start | bytes 995336 | tf_op jit(solution)/shard_map/ppermute | solution.py:514
  133.0 2.5 %collective-permute-start.27 = (bf16[144,1152]{1,0:T(8,128)(2,1)S(1)}, bf16[144,1152]{1,0:T(8,128)(2,1)S(1)}, u32[]{:S(2)}, u32[]{:S(2)}) collective-permute-start(bf16[144,1152]{1,0:T(8,128)(2,1)S(1)} %collective-permute-done.24.refs_19_), channel_id=1, source_target_pairs={{0,1},{1,0},{2,3},{3,2},{4,5},{5,4},{6,7},{7,6},{8,9},{9,8},{10,11... | collective-permute-start | bytes 995336 | tf_op jit(solution)/shard_map/ppermute | solution.py:514
  144.5 2.1 %collective-permute-start.32 = (bf16[4,2,288,128]{3,2,1,0:T(8,128)(2,1)S(1)}, bf16[4,2,288,128]{3,2,1,0:T(8,128)(2,1)S(1)}, u32[]{:S(2)}, u32[]{:S(2)}) collective-permute-start(bf16[4,2,288,128]{3,2,1,0:T(8,128)(2,1)S(1)} %get-tuple-element.83), channel_id=1, source_target_pairs={{0,1},{1,0},{2,3},{3,2},{4,5},{5,4},{6,7},{7,6},{8,9},{9,8},{10,11... | collective-permute-start | bytes 1769480 | tf_op jit(solution)/shard_map/ppermute | solution.py:514
  147.5 8.2 %collective-permute-start.33 = (bf16[288,128]{1,0:T(8,128)(2,1)S(1)}, bf16[288,128]{1,0:T(8,128)(2,1)S(1)}, u32[]{:S(2)}, u32[]{:S(2)}) collective-permute-start(bf16[288,128]{1,0:T(8,128)(2,1)S(1)} %get-tuple-element.86), channel_id=1, source_target_pairs={{0,2},{2,0},{4,6},{6,4},{8,10},{10,8},{12,14},{14,12},{1,3},{3,1},... | collective-permute-start | bytes 221192 | tf_op jit(solution)/shard_map/ppermute | solution.py:691
  149.0 8.6 %collective-permute-start.34 = (bf16[288,128]{1,0:T(8,128)(2,1)S(1)}, bf16[288,128]{1,0:T(8,128)(2,1)S(1)}, u32[]{:S(2)}, u32[]{:S(2)}) collective-permute-start(bf16[288,128]{1,0:T(8,128)(2,1)S(1)} %get-tuple-element.87), channel_id=1, source_target_pairs={{0,12},{2,14},{4,0},{6,2},{8,4},{10,6},{12,8},{14,10},{1,13},{3,15... | collective-permute-start | bytes 221192 | tf_op jit(solution)/shard_map/ppermute | solution.py:691
  151.8 6.0 %collective-permute-start.35 = (bf16[288,128]{1,0:T(8,128)(2,1)S(1)}, bf16[288,128]{1,0:T(8,128)(2,1)S(1)}, u32[]{:S(2)}, u32[]{:S(2)}) collective-permute-start(bf16[288,128]{1,0:T(8,128)(2,1)S(1)} %get-tuple-element.88), channel_id=1, source_target_pairs={{0,14},{2,12},{4,2},{6,0},{8,6},{10,4},{12,10},{14,8},{1,15},{3,13... | collective-permute-start | bytes 221192 | tf_op jit(solution)/shard_map/ppermute | solution.py:691
  151.8 11.3 %collective-permute-start.36 = (bf16[288,128]{1,0:T(8,128)(2,1)S(1)}, bf16[288,128]{1,0:T(8,128)(2,1)S(1)}, u32[]{:S(2)}, u32[]{:S(2)}) collective-permute-start(bf16[288,128]{1,0:T(8,128)(2,1)S(1)} %get-tuple-element.89), channel_id=1, source_target_pairs={{0,8},{2,10},{4,12},{6,14},{8,0},{10,2},{12,4},{14,6},{1,9},{3,11}... | collective-permute-start | bytes 221192 | tf_op jit(solution)/shard_map/ppermute | solution.py:691
  152.5 12.8 %collective-permute-start.37 = (bf16[288,128]{1,0:T(8,128)(2,1)S(1)}, bf16[288,128]{1,0:T(8,128)(2,1)S(1)}, u32[]{:S(2)}, u32[]{:S(2)}) collective-permute-start(bf16[288,128]{1,0:T(8,128)(2,1)S(1)} %get-tuple-element.90), channel_id=1, source_target_pairs={{0,10},{2,8},{4,14},{6,12},{8,2},{10,0},{12,6},{14,4},{1,11},{3,9}... | collective-permute-start | bytes 221192 | tf_op jit(solution)/shard_map/ppermute | solution.py:691
  155.6 9.6 %collective-permute-start.38 = (bf16[288,128]{1,0:T(8,128)(2,1)S(1)}, bf16[288,128]{1,0:T(8,128)(2,1)S(1)}, u32[]{:S(2)}, u32[]{:S(2)}) collective-permute-start(bf16[288,128]{1,0:T(8,128)(2,1)S(1)} %get-tuple-element.91), channel_id=1, source_target_pairs={{0,4},{2,6},{4,8},{6,10},{8,12},{10,14},{12,0},{14,2},{1,5},{3,7},... | collective-permute-start | bytes 221192 | tf_op jit(solution)/shard_map/ppermute | solution.py:691
  157.7 7.6 %collective-permute-start.39 = (bf16[288,128]{1,0:T(8,128)(2,1)S(1)}, bf16[288,128]{1,0:T(8,128)(2,1)S(1)}, u32[]{:S(2)}, u32[]{:S(2)}) collective-permute-start(bf16[288,128]{1,0:T(8,128)(2,1)S(1)} %get-tuple-element.92), channel_id=1, source_target_pairs={{0,6},{2,4},{4,10},{6,8},{8,14},{10,12},{12,2},{14,0},{1,7},{3,5},... | collective-permute-start | bytes 221192 | tf_op jit(solution)/shard_map/ppermute | solution.py:691
  (1 other events, 1.3 us)
